TPU v7x, 128 devices: a whole 4x4x4 slice. The times are simulated.
128 devices in a mesh: grp: 4 (over z), dev: 32 (over y, x, core).
Axes of the slice: x: 4, y: 4, z: 4, core: 2. Of those that a mesh axis runs over, the one named last changes fastest.
Arguments:
- adjoint_load: float32 [4096, 64, 128], P(('grp', 'dev')), as said below
- local_ops: float32 [4, 8064, 64, 64], P(None, ('grp', 'dev')), as said below
- coarse_ops: float32 [4, 4, 28, 64, 64], P(None, 'grp'), as said below
- slab_order: int32 [128, 32], P(('grp', 'dev')), may hold values from 0 to 31, each once within a row
Outputs:
- slab_adjoint: float32 [4096, 64, 128], P(('grp', 'dev'))
Inputs may be any that keep to these rules, and one draw needn't show every extreme that they name: `local_ops`: blocks of kind 3 approximate the inverses of the diagonal blocks. `coarse_ops`: same four kinds of blocks as local_ops. `adjoint_load`: real-valued right-hand sides. `slab_order`: each row lists every one of the 32 rows of one device once.
All inputs are finite; a program needn't handle non-finite values.
Results may differ from a plain program's by a relative error of at most 0.0001.
Values sent between devices are 32-bit elements; how exact they have to be, the bound alone decides.
No kernel may reach another device: no remote copies, remote signals or barrier semaphores. Data moves between devices by JAX's collectives and lax.ppermute only.
A program may use at most 64 MiB of HBM per device.

v0:
```python
import functools

import jax
import jax.numpy as jnp
from jax import lax
from jax.experimental import pallas as pl
from jax.experimental.pallas import tpu as pltpu
from jax.sharding import PartitionSpec as P


F32, BF16 = jnp.float32, jnp.bfloat16
DAMPING = 0.8
B, K = 64, 128
FINE = (32, 16, 8)
HALO = (11, 5, 2)
OWN_AT = (0, 32, 48)
CHIP = (4, 2, 1)
COARSE = (16, 8, 4)
COARSE_AT = (0, 16, 24)


def split_pair(pair, first_ref, second_ref):
    lane = lax.broadcasted_iota(jnp.int32, pair.shape, 1)
    high = pair.astype(BF16).astype(F32)
    low = pair - high
    left = lane < 64
    first_ref[...] = jnp.where(left, high, pltpu.roll(low, 64, 1)).astype(BF16)
    second_ref[...] = jnp.where(left, pltpu.roll(high, 64, 1), low).astype(BF16)


def split_row(smooth_lower, diag_upper, row_ref):
    lane = lax.broadcasted_iota(jnp.int32, smooth_lower.shape, 1)
    smooth_lower = jnp.where(lane < 64, smooth_lower * DAMPING, smooth_lower)
    split_pair(smooth_lower, row_ref.at[0:64], row_ref.at[64:128])
    split_pair(diag_upper, row_ref.at[128:192], row_ref.at[192:256])


def stack_rhs(value):
    high = value.astype(BF16)
    low = (value - high.astype(F32)).astype(BF16)
    return jnp.concatenate([high, high, low, low], axis=0)


def product(blocks, value):
    return jnp.dot(
        jnp.concatenate([blocks, blocks], axis=1), stack_rhs(value), preferred_element_type=F32
    )


def grouped(start, stop, size, body, carry=()):
    groups = (stop - start) // size
    if groups > 1:
        carry = lax.fori_loop(
            0, groups, lambda g, held: body(start + g * size, size, held), carry
        )
        start += groups * size
    while start < stop:
        count = min(size, stop - start)
        carry = body(start, count, carry)
        start += count
    return carry


def smooth(rows, q_ref, q_at, source, store, size=12):
    def body(first, count, carry):
        values = [source(first + u) for u in range(count)]
        outs = [product(q_ref[q_at + first + u, 0:64, :], values[u]) for u in range(count)]
        for u in range(count):
            store(first + u, outs[u], values[u])
        return carry

    grouped(0, rows, size, body)


def sweep(rows, q_ref, q_at, source, emit, size=13):
    def lower(k):
        return q_ref[q_at + k, 64:128, :]

    def diag(k):
        return q_ref[q_at + k, 128:192, :]

    def upper(k):
        return q_ref[q_at + k, 192:256, :]

    below = product(lower(1), source(0))
    out = product(jnp.concatenate([diag(1), lower(2)], axis=0), source(1))
    carry = (below + out[0:64], out[64:128])

    def body(first, count, carry):
        total, below = carry
        values = [source(first + u) for u in range(count)]
        outs = []
        for u in range(count):
            k = first + u
            blocks = jnp.concatenate([upper(k - 1), diag(k), lower(k + 1)], axis=0)
            outs.append(product(blocks, values[u]))
        for u in range(count):
            emit(first + u - 1, total + outs[u][0:64])
            total = outs[u][64:128] + below
            below = outs[u][128:192]
        return total, below

    total, below = grouped(2, rows - 1, size, body, carry)
    emit(rows - 2, total + product(upper(rows - 2), source(rows - 1)))


class Copies:
    def __init__(self, sems):
        self.sems, self.used = sems, 0

    def start(self, source, target):
        copy = pltpu.make_async_copy(source, target, self.sems.at[self.used])
        copy.start()
        self.used += 1
        return copy


def wait_all(copies):
    for copy in copies:
        copy.wait()


ANY = pl.BlockSpec(memory_space=pl.ANY)
SMEM = pl.BlockSpec(memory_space=pltpu.SMEM)
VMEM = pl.BlockSpec(memory_space=pltpu.VMEM)


def shape(*dims, dtype=F32):
    return jax.ShapeDtypeStruct(dims, dtype)


def split_shape(rows):
    return shape(rows, 256, 128, dtype=BF16)


def call(kernel, in_specs, out_shape, scratch=(), flops=0, size=0, room=4, aliases=None):
    return pl.pallas_call(
        kernel,
        in_specs=in_specs,
        out_specs=jax.tree.map(lambda _: VMEM, out_shape),
        out_shape=out_shape,
        scratch_shapes=list(scratch),
        input_output_aliases=aliases or {},
        cost_estimate=pl.CostEstimate(flops=flops, bytes_accessed=size, transcendentals=0),
        compiler_params=pltpu.CompilerParams(vmem_limit_bytes=room << 20),
    )


def rows_of(count):
    return pltpu.VMEM((count, B, K), F32)


def device_parity():
    return lax.rem(lax.axis_index("dev"), 2)


def pack_row(buf, i, target, at):
    target[at] = jnp.concatenate([buf[3, i], buf[0, i]], axis=1)
    target[at + 1] = jnp.concatenate([buf[1, i], buf[2, i]], axis=1)


def send_kernel(outward, ops, load, sent, buf, sems):
    parity = device_parity()
    last = parity if outward else 1 - parity
    copies = Copies(sems)
    halo = HALO[0]
    begin = (FINE[0] - halo) * last
    half = halo // 2
    first = copies.start(ops.at[:, pl.ds(begin, half)], buf.at[:, pl.ds(0, half)])
    second = copies.start(
        ops.at[:, pl.ds(begin + half, halo - half)], buf.at[:, pl.ds(half, halo - half)]
    )
    values = copies.start(load.at[pl.ds(begin, halo)], sent.at[pl.ds(2 * halo, halo)])
    first.wait()
    for i in range(halo):
        if i == half:
            second.wait()
        pack_row(buf, i, sent, 2 * i)
    values.wait()


def send_rest_kernel(ops, to_in, to_out, own, buf, sems):
    parity = device_parity()
    copies = Copies(sems)
    started = []
    for level, at in ((1, 0), (2, 5)):
        rows, halo = FINE[level], HALO[level]
        for side, last in ((0, 1 - parity), (1, parity)):
            begin = OWN_AT[level] + (rows - halo) * last
            target = buf.at[:, pl.ds(7 * side + at, halo)]
            started.append(copies.start(ops.at[:, pl.ds(begin, halo)], target))
    started.append(copies.start(ops.at[:, pl.ds(56, 7)], buf.at[:, pl.ds(14, 7)]))
    wait_all(started)

    def row(i, carry):
        pack_row(buf, i, to_in, 2 * i)
        pack_row(buf, i + 7, to_out, 2 * i)
        pack_row(buf, i + 14, own, 2 * i)
        return carry

    lax.fori_loop(0, 7, row, 0)


COARSE_IN = (1, 19, 29)


def split_rows(source, begin, rows, target, at):
    def pair_of_rows(i, carry):
        for u in range(2):
            k = begin + 2 * i + u
            split_row(
                jnp.concatenate([source[3, k], source[0, k]], axis=1),
                jnp.concatenate([source[1, k], source[2, k]], axis=1),
                target.at[at + 2 * i + u],
            )
        return carry

    lax.fori_loop(0, rows // 2, pair_of_rows, 0)


def own_kernel(ops, q0, buf, sems):
    copies = Copies(sems)
    parts = []
    for begin in (0, 16):
        part = pl.ds(begin, 16)
        parts.append(copies.start(ops.at[:, part], buf.at[:, part]))
    for begin, part in zip((0, 16), parts):
        part.wait()
        split_rows(buf, begin, 16, q0, HALO[0] + begin)


def own_rest_kernel(ops, coarse, q1, q2, qc, buf, cbuf, sems):
    copies = Copies(sems)
    loads = [
        copies.start(ops.at[:, pl.ds(32, 24)], buf),
        copies.start(coarse.at[:, 0], cbuf),
    ]
    loads[0].wait()
    split_rows(buf, 0, 16, q1, HALO[1])
    split_rows(buf, 16, 8, q2, HALO[2])
    loads[1].wait()
    for level in range(3):
        split_rows(cbuf, COARSE_AT[level], COARSE[level], qc, COARSE_IN[level])


def halo_kernel(levels, got_in, got_out, *refs):
    parity = device_parity()
    targets = refs[len(levels):]
    at = 0
    for level, target in zip(levels, targets):
        rows, halo = FINE[level], HALO[level]
        for got, right in ((got_in, 1 - parity), (got_out, parity)):
            begin = (rows + halo) * right

            def row(i, carry):
                split_row(got[2 * (at + i)], got[2 * (at + i) + 1], target.at[begin + i])
                return carry

            lax.fori_loop(0, halo, row, 0)
        at += halo


CHIP_AT = (0, 4, 6)
CHIPQ_AT = (0, 24, 36)
CHIPQ_ROWS = 42


def chip_slots(parity):
    return (
        (0, 0, 2 + parity),
        (1, 0, 3 - parity),
        (2, 0, 1 + 3 * parity),
        (2, 1, 5 * parity),
        (3, 0, 4 - 3 * parity),
        (3, 1, 5 - 5 * parity),
    )


def chip_send_kernel(own, partner, both):
    near = device_parity()

    def own_row(i, carry):
        both[i] = own[i]
        return carry

    lax.fori_loop(0, 14, own_row, 0)
    for i in range(3):
        for u in range(2):
            both[14 + 2 * i + u] = partner[2 * (near + i) + u]
    for u in range(2):
        both[20 + u] = partner[2 * (CHIP_AT[1] + near) + u]


def chip_kernel(own, partner, mine, theirs, q_chip):
    parity = device_parity()
    arrays = (own, partner, mine, theirs)
    for which, offset, slot in chip_slots(parity):
        if offset:
            near = 1 - parity if which == 2 else parity
            moves = [(14 + 2 * i, 4 * slot + near + i) for i in range(3)]
            moves.append((20, CHIPQ_AT[1] + 2 * slot + near))
        else:
            moves = [
                (2 * (CHIP_AT[level] + i), CHIPQ_AT[level] + slot * CHIP[level] + i)
                for level in range(3)
                for i in range(CHIP[level])
            ]
        for at, target in moves:
            split_row(arrays[which][at], arrays[which][at + 1], q_chip.at[target])


def restrict(r, target, rows, shift):
    def body(first, count, carry):
        for u in range(count):
            i = first + u
            target[i] = 0.5 * (r[2 * i + shift] + r[2 * i + shift + 1])
        return carry

    grouped(0, rows, 4, body)


def residual_into(r, b):
    def emit(k, value):
        r[k - 1] = b[k] - value

    return emit


def down_fine_kernel(at, load, load_in, load_out, q0, x0, b0, b1, r):
    parity = device_parity()
    rows, halo = FINE[0], HALO[0]
    for source, shift, count, begin in (
        (load, 0, rows, halo),
        (load_in, at, halo, (rows + halo) * (1 - parity)),
        (load_out, at, halo, (rows + halo) * parity),
    ):

        def keep(i, value, given):
            x0[begin + i] = value
            b0[begin + i] = given

        smooth(count, q0, begin, lambda i: source[shift + i], keep)
    sweep(54, q0, 0, lambda k: x0[k], residual_into(r, b0))
    restrict(r, b1, 26, 0)


def level_down(rows, q, q_at, b, x, r):
    def keep(i, value, given):
        x[i] = value

    smooth(rows, q, q_at, lambda i: b[i], keep)
    sweep(rows, q, q_at, lambda k: x[k], residual_into(r, b))


def down_kernel(b1, q1, q2, x1, x2, b2, b3, r):
    level_down(26, q1, 0, b1, x1, r)
    restrict(r, b2, 12, 0)
    level_down(12, q2, 0, b2, x2, r)
    restrict(r, b3, 4, 1)


def chip_down_kernel(own, partner, mine, theirs, q, c6, c6_x5, x3, b3, x4, b4, x5, b5, r):
    parity = device_parity()
    arrays = (own, partner, mine, theirs)
    for which, offset, slot in chip_slots(parity):
        for i in range(4):
            b3[4 * slot + i] = arrays[which][4 * offset + i]

    def keep(i, value, given):
        x3[i] = value

    smooth(22, q, 1, lambda i: b3[i + 1], keep)

    def emit(k, value):
        r[k - 1] = b3[k + 1] - value

    sweep(22, q, 1, lambda k: x3[k], emit)
    restrict(r, b4, 10, 0)
    level_down(10, q, CHIPQ_AT[1] + 1, b4, x4, r)
    restrict(r, b5, 4, 0)
    level_down(4, q, CHIPQ_AT[2] + 1, b5, x5, r)
    mean = 0.5 * (r[0] + r[1])
    c6[0] = mean
    c6_x5[0] = mean
    c6_x5[1] = x5[1 + parity]


def row_kernel(own, ahead, across, behind, row, row_x5):
    for i, part in enumerate((own, ahead, across, behind)):
        row[i] = part[0]
        row_x5[i] = part[0]

    @pl.when(device_parity() == 0)
    def _():
        row_x5[4] = ahead[1]

    @pl.when(device_parity() == 1)
    def _():
        row_x5[4] = behind[1]


def up_kernel(last, *refs):
    refs = list(refs)

    def take(count):
        taken = refs[:count]
        del refs[:count]
        return taken

    order = take(1)[0] if last else None
    gathered = take(4)
    x5, b5, x4, b4, x3, b3, x2, b2, x1, b1, x0, b0, qc, qk, q2, q1, q0 = take(17)
    sums = take(1)[0] if last else None
    outs = take(4)
    xc, bc, xk5, f, g, xp, r = refs
    position = lax.axis_index("dev")
    parity, chip = lax.rem(position, 2), lax.div(position, 2)
    row_y, row_x = lax.div(chip, 4), lax.rem(chip, 4)

    for sy in range(4):
        for sx in range(4):
            place = 4 * lax.rem(row_y + 4 - sy, 4) + lax.rem(row_x + 4 - sx, 4)
            bc[1 + place] = gathered[sy][sx]
    zero = jnp.zeros((B, K), F32)
    for level in range(3):
        for edge in (COARSE_IN[level] - 1, COARSE_IN[level] + COARSE[level]):
            xc[edge] = zero

    for level in range(3):
        rows, base = COARSE[level], COARSE_IN[level]

        def keep(i, value, given):
            xc[base + i] = value

        smooth(rows, qc, base, lambda i: bc[base + i], keep)
        if level == 2:
            break

        def emit(k, value):
            r[k - 1] = bc[base - 1 + k] - value

        sweep(rows + 2, qc, base - 1, lambda k: xc[base - 1 + k], emit)
        following = COARSE_IN[level + 1]
        for i in range(rows // 2):
            bc[following + i] = 0.5 * (r[2 * i] + r[2 * i + 1])

    for level in (2, 1, 0):
        rows, base = COARSE[level], COARSE_IN[level]
        if level < 2:
            below = COARSE_IN[level + 1]
            for i in range(rows):
                xc[base + i] = xc[base + i] + xc[below + i // 2]

        def emit(k, value):
            r[k - 1] = bc[base - 1 + k] - value

        sweep(rows + 2, qc, base - 1, lambda k: xc[base - 1 + k], emit)

        def keep(i, value, given):
            xc[base + i] = xc[base + i] + value

        smooth(rows, qc, base, lambda i: r[i], keep)

    def post(rows, q, q_at, right_side, b_at, target):
        def emit(k, value):
            r[k - 1] = right_side[b_at + k - 1] - value

        sweep(rows + 4, q, q_at, lambda k: xp[k], emit)

        def keep(i, value, given):
            target[i] = xp[i + 1] + value

        smooth(rows + 2, q, q_at + 1, lambda i: r[i], keep)

    def correct(rows, values, x_at, source):
        def body(first, count, carry):
            for u in range(count):
                j = first + u
                value = source[j]
                xp[2 * j] = values[x_at + 2 * j] + value
                xp[2 * j + 1] = values[x_at + 2 * j + 1] + value
            return carry

        grouped(0, rows // 2 + 2, 3, body)

    for i in range(4):
        xk5[1 + i] = x5[i]
    inside = row_x != 3 * parity
    outermost = chip == 15 * parity

    @pl.when(inside)
    def _():
        xk5[5 * parity] = gathered[0][4]

    @pl.when(jnp.logical_not(inside) & (parity == 0))
    def _():
        xk5[0] = gathered[1][4]

    @pl.when(jnp.logical_not(inside) & (parity == 1))
    def _():
        xk5[5] = gathered[3][4]

    @pl.when(outermost)
    def _():
        xk5[5 * parity] = zero

    for k in range(5):
        xp[k] = xk5[k + parity] + xc[chip + lax.div(k + parity, 2)]
    post(1, qk, CHIPQ_AT[2] + parity, b5, parity, f)
    correct(2, x4, 1 + 2 * parity, f)
    post(2, qk, CHIPQ_AT[1] + 2 + 2 * parity, b4, 2 + 2 * parity, g)
    correct(4, x3, 5 + 4 * parity, g)
    post(4, qk, 6 + 4 * parity, b3, 7 + 4 * parity, f)
    correct(8, x2, 0, f)
    post(8, q2, 0, b2, 1, g)
    correct(16, x1, 3, g)
    post(16, q1, 3, b1, 4, f)
    correct(32, x0, 9, f)
    post(32, q0, 9, b0, 10, g)

    if last:
        group = lax.axis_index("grp")
        for s in range(4):
            base = 8 * lax.rem(group + s, 4)
            for u in range(8):
                pick = order[0, base + u]
                outs[s][u] = sums[pick] + g[pick + 1]
        return
    first_out, load_next, next_in, next_out = outs

    def emit(k, value):
        load_next[k - 1] = b0[k + 10] - value
        first_out[k - 1] = g[k]

    sweep(34, q0, 10, lambda k: g[k], emit)

    def edge_row(i, carry):
        next_in[i] = load_next[21 * (1 - parity) + i]
        next_out[i] = load_next[21 * parity + i]
        return carry

    lax.fori_loop(0, 11, edge_row, 0)


def place_kernel(part0, part1, part2, part3, out, sems):
    copies = Copies(sems)
    started = []
    group = lax.axis_index("grp")
    for s, part in enumerate((part0, part1, part2, part3)):
        begin = 8 * lax.rem(group + 4 - s, 4)
        started.append(copies.start(part, out.at[pl.ds(begin, 8)]))
    wait_all(started)


def shards(adjoint_load, local_ops, coarse_ops, slab_order):
    devices = lax.axis_size("dev")
    side = 4

    def swap_in(value):
        return lax.ppermute(value, "dev", [(i, i ^ 1) for i in range(devices)])

    def swap_out(value):
        route = []
        for i in range(1, devices - 1, 2):
            route += [(i, i + 1), (i + 1, i)]
        return lax.ppermute(value, "dev", route)

    def around(value):
        partner = swap_in(value)
        mine = swap_out(jnp.concatenate([value, partner], axis=0))
        theirs = swap_in(mine)
        return value, partner, mine, theirs

    def shift(value, along_y, step):
        route = []
        for i in range(devices):
            y, x, core = i // (2 * side), i // 2 % side, i % 2
            if along_y:
                y = (y + step) % side
            else:
                x = (x + step) % side
            route.append((i, (y * side + x) * 2 + core))
        return lax.ppermute(value, "dev", route)

    def gather(c6, c6_x5):
        parts = (c6_x5, shift(c6_x5, False, 1), shift(c6, False, 2), shift(c6_x5, False, 3))
        row, row_x5 = call(
            row_kernel, [VMEM] * 4, [shape(4, B, K), shape(5, B, K)], size=1 << 18
        )(*parts)
        return [row_x5, shift(row_x5, True, 1), shift(row, True, 2), shift(row_x5, True, 3)]

    halo = HALO[0]

    def send(outward):
        return call(
            functools.partial(send_kernel, outward), [ANY, ANY], shape(3 * halo, B, K),
            [pltpu.VMEM((4, halo, B, B), F32), pltpu.SemaphoreType.DMA((3,))], size=4 << 20, room=58,
        )(local_ops, adjoint_load)

    got_out = swap_out(send(True))
    got_in = swap_in(send(False))
    rest_in, rest_out, own7 = call(
        send_rest_kernel, [ANY], [shape(14, B, K)] * 3,
        [pltpu.VMEM((4, 21, B, B), F32), pltpu.SemaphoreType.DMA((5,))], size=4 << 20, room=50,
    )(local_ops)
    more_out = swap_out(rest_out)
    more_in = swap_in(rest_in)
    q0 = call(
        own_kernel, [ANY], [split_shape(54)],
        [pltpu.VMEM((4, 32, B, B), F32), pltpu.SemaphoreType.DMA((2,))], size=8 << 20, room=40,
    )(local_ops)[0]
    q1, q2, qc = call(
        own_rest_kernel, [ANY, ANY], [split_shape(26), split_shape(12), split_shape(34)],
        [pltpu.VMEM((4, 24, B, B), F32), pltpu.VMEM((4, 28, B, B), F32), pltpu.SemaphoreType.DMA((2,))],
        size=12 << 20, room=24,
    )(local_ops, coarse_ops)
    q0 = call(
        functools.partial(halo_kernel, (0,)), [VMEM] * 3, [split_shape(54)],
        size=4 << 20, aliases={2: 0},
    )(got_in, got_out, q0)[0]
    q1, q2 = call(
        functools.partial(halo_kernel, (1, 2)), [VMEM] * 4, [split_shape(26), split_shape(12)],
        size=4 << 20, aliases={2: 0, 3: 1},
    )(more_in, more_out, q1, q2)
    partner7 = swap_in(own7)
    both = call(chip_send_kernel, [VMEM] * 2, shape(22, B, K), size=2 << 20)(own7, partner7)
    both = lax.optimization_barrier((both, q0))[0]
    mine = swap_out(both)
    q_chip = call(
        chip_kernel, [VMEM] * 4, split_shape(CHIPQ_ROWS), size=6 << 20,
    )(own7, partner7, mine, swap_in(mine))

    def cycle(at, load, load_in, load_out, earlier=None):
        last = earlier is not None
        x0, b0, b1 = call(
            functools.partial(down_fine_kernel, at),
            [VMEM] * 4, [shape(54, B, K), shape(54, B, K), shape(26, B, K)],
            [rows_of(52)], flops=54 * 4 * 2 * 64 * 256 * 128, size=16 << 20,
        )(load, load_in, load_out, q0)
        x1, x2, b2, b3 = call(
            down_kernel,
            [VMEM] * 3, [shape(26, B, K), shape(12, B, K), shape(12, B, K), shape(4, B, K)],
            [rows_of(24)], flops=38 * 4 * 2 * 64 * 256 * 128, size=8 << 20,
        )(b1, q1, q2)
        c6, c6_x5, x3, b3c, x4, b4, x5, b5 = call(
            chip_down_kernel, [VMEM] * 5,
            [shape(1, B, K), shape(2, B, K), shape(22, B, K), shape(24, B, K), shape(10, B, K), shape(10, B, K),
             shape(4, B, K), shape(4, B, K)],
            [rows_of(20)], flops=36 * 4 * 2 * 64 * 256 * 128, size=6 << 20,
        )(*around(b3), q_chip)
        operands = ([slab_order] if last else []) + gather(c6, c6_x5)
        operands += [x5, b5, x4, b4, x3, b3c, x2, b2, x1, b1, x0, b0, qc, q_chip, q2, q1, q0]
        operands += [earlier] if last else []
        out_shape = [shape(8, B, K)] * 4 if last else [shape(32, B, K)] * 2 + [shape(11, B, K)] * 2
        return call(
            functools.partial(up_kernel, last),
            ([SMEM] if last else []) + [VMEM] * (len(operands) - last), out_shape,
            [rows_of(34), rows_of(34), rows_of(6), rows_of(34), rows_of(34), rows_of(36), rows_of(34)],
            flops=130 * 4 * 2 * 64 * 256 * 128, size=20 << 20, room=9,
        )(*operands)

    first, load_next, next_in, next_out = cycle(2 * halo, adjoint_load, got_in, got_out)
    load_out = swap_out(next_out)
    load_in = swap_in(next_in)
    parts = cycle(0, load_next, load_in, load_out, first)

    groups = lax.axis_size("grp")
    arrived = [parts[0]]
    for s in range(1, groups):
        arrived.append(lax.ppermute(parts[s], "grp", [(i, (i + s) % groups) for i in range(groups)]))
    return pl.pallas_call(
        place_kernel, name="place", in_specs=[VMEM] * 4, out_specs=ANY, out_shape=shape(32, B, K),
        scratch_shapes=[pltpu.SemaphoreType.DMA((4,))],
        compiler_params=pltpu.CompilerParams(vmem_limit_bytes=4 << 20),
    )(*arrived)


def solution(mesh):
    placed = (
        P(("grp", "dev"), None, None),
        P(None, ("grp", "dev"), None, None),
        P(None, "grp", None, None, None),
        P(("grp", "dev"), None),
    )

    return jax.shard_map(
        shards, mesh=mesh, in_specs=placed, out_specs=P(("grp", "dev"), None, None), check_vma=False
    )
```

profile of v0, /device:TPU:0, one launch (start us, length us, event | category | flops | bytes accessed | tf_op | source)
XLA Modules:
  0.0 166.2 jit_solution(369829359749044368)
XLA Ops:
  0.0 2.5 %shard_map.47 = f32[33,64,128]{2,1,0:T(8,128)} custom-call(f32[4,63,64,64]{3,2,1,0:T(8,128)} %ops.9, f32[32,64,128]{2,1,0:T(8,128)} %load.5), custom_call_target="tpu_custom_call" | custom-call | bytes 4194304 | tf_op jit(solution)/shard_map/pallas_call | solution.py:595
  3.3 2.5 %shard_map.46 = f32[33,64,128]{2,1,0:T(8,128)} custom-call(f32[4,63,64,64]{3,2,1,0:T(8,128)} %ops.9, f32[32,64,128]{2,1,0:T(8,128)} %load.5), custom_call_target="tpu_custom_call" | custom-call | bytes 4194304 | tf_op jit(solution)/shard_map/pallas_call | solution.py:595
  5.8 3.0 %collective-permute-start = (f32[33,64,128]{2,1,0:T(8,128)}, f32[33,64,128]{2,1,0:T(8,128)S(1)}, u32[]{:S(2)}, u32[]{:S(2)}) collective-permute-start(f32[33,64,128]{2,1,0:T(8,128)} %shard_map.46), channel_id=1, source_target_pairs={{0,1},{1,0},{2,3},{3,2},{4,5},{5,4},{6,7},{7,6},{8,9},{9,8},{10,11... | collective-permute-start | bytes 3244040 | tf_op jit(solution)/shard_map/ppermute | solution.py:560
  8.8 2.7 %shard_map.51 = (f32[14,64,128]{2,1,0:T(8,128)S(1)}, f32[14,64,128]{2,1,0:T(8,128)S(1)}, f32[14,64,128]{2,1,0:T(8,128)S(1)}) custom-call(f32[4,63,64,64]{3,2,1,0:T(8,128)} %ops.9), custom_call_target="tpu_custom_call" | custom-call | bytes 4194304 | tf_op jit(solution)/shard_map/pallas_call | solution.py:602
  13.0 3.5 %shard_map.48.refs_0_ = bf16[54,256,128]{2,1,0:T(8,128)(2,1)S(1)} custom-call(f32[4,63,64,64]{3,2,1,0:T(8,128)S(1)} %copy-done), custom_call_target="tpu_custom_call" | custom-call | bytes 8388608 | tf_op jit(solution)/shard_map/pallas_call | solution.py:608
  16.6 2.0 %shard_map.49.q0.refs_20_.refs_21_ = bf16[54,256,128]{2,1,0:T(8,128)(2,1)S(1)} custom-call(f32[33,64,128]{2,1,0:T(8,128)S(1)} %collective-permute-done.got_in.load_in, f32[33,64,128]{2,1,0:T(8,128)S(1)} %collective-permute-done.1.got_out.load_out, bf16[54,256,128]{2,1,0:T(8,128)(2,1)S(1)} %shard_map.48.refs_0_), custom_call_target="tpu_custom_call", output_to_operand_aliasing={{}: (2, {})} | custom-call | bytes 4194304 | tf_op jit(solution)/shard_map/pallas_call | solution.py:617
  19.4 5.6 %collective-permute-start.2 = (f32[14,64,128]{2,1,0:T(8,128)S(1)}, f32[14,64,128]{2,1,0:T(8,128)S(1)}, u32[]{:S(2)}, u32[]{:S(2)}) collective-permute-start(f32[14,64,128]{2,1,0:T(8,128)S(1)} %get-tuple-element.57), channel_id=1, source_target_pairs={{0,1},{1,0},{2,3},{3,2},{4,5},{5,4},{6,7},{7,6},{8,9},{9,8},{10,11... | collective-permute-start | bytes 1376264 | tf_op jit(solution)/shard_map/ppermute | solution.py:560
  25.7 5.6 %shard_map.52 = (bf16[26,256,128]{2,1,0:T(8,128)(2,1)S(1)}, bf16[12,256,128]{2,1,0:T(8,128)(2,1)S(1)}, bf16[34,256,128]{2,1,0:T(8,128)(2,1)S(1)}) custom-call(f32[4,63,64,64]{3,2,1,0:T(8,128)S(1)} %copy-done, f32[4,1,28,64,64]{4,3,2,1,0:T(8,128)S(1)} %copy-done.2), custom_call_target="tpu_custom_call" | custom-call | bytes 12582912 | tf_op jit(solution)/shard_map/pallas_call | solution.py:612
  32.6 3.1 %shard_map.50 = (f32[54,64,128]{2,1,0:T(8,128)S(1)}, f32[54,64,128]{2,1,0:T(8,128)S(1)}, f32[26,64,128]{2,1,0:T(8,128)S(1)}) custom-call(f32[32,64,128]{2,1,0:T(8,128)S(1)} %copy-done.1, f32[33,64,128]{2,1,0:T(8,128)S(1)} %collective-permute-done.got_in.load_in, f32[33,64,128]{2,1,0:T(8,128)S(1)} %collective-permute-done.1.got_out.load_out, ...), custom_call_target="tpu_custom_call" | custom-call | flops 905969664 | bytes 16777216 | tf_op jit(solution)/shard_map/pallas_call | solution.py:635
  35.7 2.0 %shard_map.54 = (f32[26,64,128]{2,1,0:T(8,128)S(1)}, f32[12,64,128]{2,1,0:T(8,128)S(1)}, f32[12,64,128]{2,1,0:T(8,128)S(1)}, f32[4,64,128]{2,1,0:T(8,128)S(1)}) custom-call(f32[26,64,128]{2,1,0:T(8,128)S(1)} %get-tuple-element.56.b1.refs_13_, bf16[26,256,128]{2,1,0:T(8,128)(2,1)S(1)} %get-tuple-element.61.q1.refs_19_.refs_20_, ...), custom_call_target="tpu_custom_call" | custom-call | flops 637534208 | bytes 8388608 | tf_op jit(solution)/shard_map/pallas_call | solution.py:640
  37.7 7.5 %collective-permute-start.4 = (f32[4,64,128]{2,1,0:T(8,128)S(1)}, f32[4,64,128]{2,1,0:T(8,128)S(1)}, u32[]{:S(2)}, u32[]{:S(2)}) collective-permute-start(f32[4,64,128]{2,1,0:T(8,128)S(1)} %get-tuple-element.63.own), channel_id=1, source_target_pairs={{0,1},{1,0},{2,3},{3,2},{4,5},{5,4},{6,7},{7,6},{8,9},{9,8},{10,11... | collective-permute-start | bytes 393224 | tf_op jit(solution)/shard_map/ppermute | solution.py:560
  46.9 7.4 %collective-permute-start.6 = (f32[8,64,128]{2,1,0:T(8,128)S(1)}, f32[8,64,128]{2,1,0:T(8,128)S(1)}, u32[]{:S(2)}, u32[]{:S(2)}) collective-permute-start(f32[8,64,128]{2,1,0:T(8,128)S(1)} %collective-permute-done.5.mine), channel_id=1, source_target_pairs={{0,1},{1,0},{2,3},{3,2},{4,5},{5,4},{6,7},{7,6},{8,9},{9,8},{10,11... | collective-permute-start | bytes 786440 | tf_op jit(solution)/shard_map/ppermute | solution.py:560
  57.3 9.1 %collective-permute-start.12 = (f32[2,64,128]{2,1,0:T(8,128)S(1)}, f32[2,64,128]{2,1,0:T(8,128)S(1)}, u32[]{:S(2)}, u32[]{:S(2)}) collective-permute-start(f32[2,64,128]{2,1,0:T(8,128)S(1)} %get-tuple-element.66.own), channel_id=1, source_target_pairs={{0,6},{1,7},{2,0},{3,1},{4,2},{5,3},{6,4},{7,5},{8,14},{9,15},{10,... | collective-permute-start | bytes 196616 | tf_op jit(solution)/shard_map/ppermute | solution.py:583
  68.0 3.9 %collective-permute-done.11.across = f32[1,64,128]{2,1,0:T(8,128)S(1)} collective-permute-done((f32[1,64,128]{2,1,0:T(8,128)S(1)}, f32[1,64,128]{2,1,0:T(8,128)S(1)}, u32[]{:S(2)}, u32[]{:S(2)}) %collective-permute-start.11) | collective-permute-done | bytes 32800 | tf_op jit(solution)/shard_map/ppermute | solution.py:583
  72.5 2.3 %collective-permute-start.15 = (f32[5,64,128]{2,1,0:T(8,128)S(1)}, f32[5,64,128]{2,1,0:T(8,128)S(1)}, u32[]{:S(2)}, u32[]{:S(2)}) collective-permute-start(f32[5,64,128]{2,1,0:T(8,128)S(1)} %get-tuple-element.68.refs_0_), channel_id=1, source_target_pairs={{0,24},{1,25},{2,26},{3,27},{4,28},{5,29},{6,30},{7,31},{8,0},{9,1... | collective-permute-start | bytes 491528 | tf_op jit(solution)/shard_map/ppermute | solution.py:583
  74.8 3.0 %collective-permute-start.14 = (f32[4,64,128]{2,1,0:T(8,128)S(1)}, f32[4,64,128]{2,1,0:T(8,128)S(1)}, u32[]{:S(2)}, u32[]{:S(2)}) collective-permute-start(f32[4,64,128]{2,1,0:T(8,128)S(1)} %get-tuple-element.69), channel_id=1, source_target_pairs={{0,16},{1,17},{2,18},{3,19},{4,20},{5,21},{6,22},{7,23},{8,24},{9,... | collective-permute-start | bytes 393224 | tf_op jit(solution)/shard_map/ppermute | solution.py:583
  77.8 6.3 %collective-permute-done.14.refs_2_ = f32[4,64,128]{2,1,0:T(8,128)S(1)} collective-permute-done((f32[4,64,128]{2,1,0:T(8,128)S(1)}, f32[4,64,128]{2,1,0:T(8,128)S(1)}, u32[]{:S(2)}, u32[]{:S(2)}) %collective-permute-start.14) | collective-permute-done | bytes 131104 | tf_op jit(solution)/shard_map/ppermute | solution.py:583
  84.1 9.0 %shard_map.59 = (f32[32,64,128]{2,1,0:T(8,128)S(1)}, f32[32,64,128]{2,1,0:T(8,128)S(1)}, f32[11,64,128]{2,1,0:T(8,128)S(1)}, f32[11,64,128]{2,1,0:T(8,128)S(1)}) custom-call(f32[5,64,128]{2,1,0:T(8,128)S(1)} %get-tuple-element.68.refs_0_, f32[5,64,128]{2,1,0:T(8,128)S(1)} %collective-permute-done.13.refs_1_, ...), custom_call_target="tpu_custom_call" | custom-call | flops 2181038080 | bytes 20971520 | tf_op jit(solution)/shard_map/pallas_call | solution.py:655
  94.8 3.1 %shard_map.60 = (f32[54,64,128]{2,1,0:T(8,128)S(1)}, f32[54,64,128]{2,1,0:T(8,128)S(1)}, f32[26,64,128]{2,1,0:T(8,128)S(1)}) custom-call(f32[32,64,128]{2,1,0:T(8,128)S(1)} %get-tuple-element.82.load, f32[11,64,128]{2,1,0:T(8,128)S(1)} %collective-permute-done.16.load_in, f32[11,64,128]{2,1,0:T(8,128)S(1)} %collective-permute-done.17.load_out, ...), custom_call_target="tpu_custom_call" | custom-call | flops 905969664 | bytes 16777216 | tf_op jit(solution)/shard_map/pallas_call | solution.py:635
  97.9 2.0 %shard_map.61 = (f32[26,64,128]{2,1,0:T(8,128)S(1)}, f32[12,64,128]{2,1,0:T(8,128)S(1)}, f32[12,64,128]{2,1,0:T(8,128)S(1)}, f32[4,64,128]{2,1,0:T(8,128)S(1)}) custom-call(f32[26,64,128]{2,1,0:T(8,128)S(1)} %get-tuple-element.85.b1.refs_14_, bf16[26,256,128]{2,1,0:T(8,128)(2,1)S(1)} %get-tuple-element.61.q1.refs_19_.refs_20_, ...), custom_call_target="tpu_custom_call" | custom-call | flops 637534208 | bytes 8388608 | tf_op jit(solution)/shard_map/pallas_call | solution.py:640
  99.9 7.6 %collective-permute-start.18 = (f32[4,64,128]{2,1,0:T(8,128)S(1)}, f32[4,64,128]{2,1,0:T(8,128)S(1)}, u32[]{:S(2)}, u32[]{:S(2)}) collective-permute-start(f32[4,64,128]{2,1,0:T(8,128)S(1)} %get-tuple-element.86.own), channel_id=1, source_target_pairs={{0,1},{1,0},{2,3},{3,2},{4,5},{5,4},{6,7},{7,6},{8,9},{9,8},{10,11... | collective-permute-start | bytes 393224 | tf_op jit(solution)/shard_map/ppermute | solution.py:560
  109.3 7.4 %collective-permute-start.20 = (f32[8,64,128]{2,1,0:T(8,128)S(1)}, f32[8,64,128]{2,1,0:T(8,128)S(1)}, u32[]{:S(2)}, u32[]{:S(2)}) collective-permute-start(f32[8,64,128]{2,1,0:T(8,128)S(1)} %collective-permute-done.19.mine), channel_id=1, source_target_pairs={{0,1},{1,0},{2,3},{3,2},{4,5},{5,4},{6,7},{7,6},{8,9},{9,8},{10,11... | collective-permute-start | bytes 786440 | tf_op jit(solution)/shard_map/ppermute | solution.py:560
  117.8 1.9 %shard_map.62 = (f32[1,64,128]{2,1,0:T(8,128)S(1)}, f32[2,64,128]{2,1,0:T(8,128)S(1)}, f32[22,64,128]{2,1,0:T(8,128)S(1)}, f32[24,64,128]{2,1,0:T(8,128)S(1)}, f...) custom-call(f32[4,64,128]{2,1,0:T(8,128)S(1)} %get-tuple-element.86., ...), custom_call_target="tpu_custom_call" | custom-call | flops 603979776 | bytes 6291456 | tf_op jit(solution)/shard_map/pallas_call | solution.py:645
  119.7 5.9 %collective-permute-start.23 = (f32[2,64,128]{2,1,0:T(8,128)S(1)}, f32[2,64,128]{2,1,0:T(8,128)S(1)}, u32[]{:S(2)}, u32[]{:S(2)}) collective-permute-start(f32[2,64,128]{2,1,0:T(8,128)S(1)} %get-tuple-element.87.own), channel_id=1, source_target_pairs={{0,6},{1,7},{2,0},{3,1},{4,2},{5,3},{6,4},{7,5},{8,14},{9,15},{10,... | collective-permute-start | bytes 196616 | tf_op jit(solution)/shard_map/ppermute | solution.py:583
  127.1 3.9 %collective-permute-done.22.across = f32[1,64,128]{2,1,0:T(8,128)S(1)} collective-permute-done((f32[1,64,128]{2,1,0:T(8,128)S(1)}, f32[1,64,128]{2,1,0:T(8,128)S(1)}, u32[]{:S(2)}, u32[]{:S(2)}) %collective-permute-start.22) | collective-permute-done | bytes 32800 | tf_op jit(solution)/shard_map/ppermute | solution.py:583
  131.8 1.9 %collective-permute-start.24 = (f32[5,64,128]{2,1,0:T(8,128)S(1)}, f32[5,64,128]{2,1,0:T(8,128)S(1)}, u32[]{:S(2)}, u32[]{:S(2)}) collective-permute-start(f32[5,64,128]{2,1,0:T(8,128)S(1)} %get-tuple-element.89.refs_1_), channel_id=1, source_target_pairs={{0,8},{1,9},{2,10},{3,11},{4,12},{5,13},{6,14},{7,15},{8,16},{9,17... | collective-permute-start | bytes 491528 | tf_op jit(solution)/shard_map/ppermute | solution.py:583
  135.0 6.3 %collective-permute-done.25.refs_3_ = f32[4,64,128]{2,1,0:T(8,128)S(1)} collective-permute-done((f32[4,64,128]{2,1,0:T(8,128)S(1)}, f32[4,64,128]{2,1,0:T(8,128)S(1)}, u32[]{:S(2)}, u32[]{:S(2)}) %collective-permute-start.25) | collective-permute-done | bytes 131104 | tf_op jit(solution)/shard_map/ppermute | solution.py:583
  141.5 8.2 %shard_map.64 = (f32[8,64,128]{2,1,0:T(8,128)S(1)}, f32[8,64,128]{2,1,0:T(8,128)S(1)}, f32[8,64,128]{2,1,0:T(8,128)S(1)}, f32[8,64,128]{2,1,0:T(8,128)S(1)}) custom-call(s32[1,32]{1,0:T(1,128)S(1)} %copy-done.3, f32[5,64,128]{2,1,0:T(8,128)S(1)} %get-tuple-element.89.refs_1_, f32[5,64,128]{2,1,0:T(8,128)S(1)} %collective-permute-done.24.refs_2_, ...), custom_call_target="tpu_custom_call" | custom-call | flops 2181038080 | bytes 20971520 | tf_op jit(solution)/shard_map/pallas_call | solution.py:655
  149.7 2.0 %collective-permute-start.27 = (f32[8,64,128]{2,1,0:T(8,128)S(1)}, f32[8,64,128]{2,1,0:T(8,128)S(1)}, u32[]{:S(2)}, u32[]{:S(2)}) collective-permute-start(f32[8,64,128]{2,1,0:T(8,128)S(1)} %get-tuple-element.104), channel_id=1, source_target_pairs={{0,32},{32,64},{64,96},{96,0},{1,33},{33,65},{65,97},{97,1},{2,34}... | collective-permute-start | bytes 786440 | tf_op jit(solution)/shard_map/ppermute | solution.py:670
  151.7 3.6 %collective-permute-start.28 = (f32[8,64,128]{2,1,0:T(8,128)S(1)}, f32[8,64,128]{2,1,0:T(8,128)S(1)}, u32[]{:S(2)}, u32[]{:S(2)}) collective-permute-start(f32[8,64,128]{2,1,0:T(8,128)S(1)} %get-tuple-element.105), channel_id=1, source_target_pairs={{0,64},{32,96},{64,0},{96,32},{1,65},{33,97},{65,1},{97,33},{2,66}... | collective-permute-start | bytes 786440 | tf_op jit(solution)/shard_map/ppermute | solution.py:670
  156.3 3.8 %collective-permute-done.27.part1 = f32[8,64,128]{2,1,0:T(8,128)S(1)} collective-permute-done((f32[8,64,128]{2,1,0:T(8,128)S(1)}, f32[8,64,128]{2,1,0:T(8,128)S(1)}, u32[]{:S(2)}, u32[]{:S(2)}) %collective-permute-start.27) | collective-permute-done | bytes 262176 | tf_op jit(solution)/shard_map/ppermute | solution.py:670
  160.0 5.0 %collective-permute-done.28.part2 = f32[8,64,128]{2,1,0:T(8,128)S(1)} collective-permute-done((f32[8,64,128]{2,1,0:T(8,128)S(1)}, f32[8,64,128]{2,1,0:T(8,128)S(1)}, u32[]{:S(2)}, u32[]{:S(2)}) %collective-permute-start.28) | collective-permute-done | bytes 262176 | tf_op jit(solution)/shard_map/ppermute | solution.py:670
  (58 shorter events, 22.3 us)
Async XLA Ops:
  2.5 14.0 %collective-permute-start.1 = (f32[33,64,128]{2,1,0:T(8,128)}, f32[33,64,128]{2,1,0:T(8,128)S(1)}, u32[]{:S(2)}, u32[]{:S(2)}) collective-permute-start(f32[33,64,128]{2,1,0:T(8,128)} %shard_map.47), channel_id=1, source_target_pairs={{1,2},{2,1},{3,4},{4,3},{5,6},{6,5},{7,8},{8,7},{9,10},{10,9},{11,... | collective-permute-start | bytes 3244040 | tf_op jit(solution)/shard_map/ppermute | solution.py:566
  5.8 10.8 %collective-permute-start = (f32[33,64,128]{2,1,0:T(8,128)}, f32[33,64,128]{2,1,0:T(8,128)S(1)}, u32[]{:S(2)}, u32[]{:S(2)}) collective-permute-start(f32[33,64,128]{2,1,0:T(8,128)} %shard_map.46), channel_id=1, source_target_pairs={{0,1},{1,0},{2,3},{3,2},{4,5},{5,4},{6,7},{7,6},{8,9},{9,8},{10,11... | collective-permute-start | bytes 3244040 | tf_op jit(solution)/shard_map/ppermute | solution.py:560
  11.6 4.9 %collective-permute-start.7 = (f32[14,64,128]{2,1,0:T(8,128)S(1)}, f32[14,64,128]{2,1,0:T(8,128)S(1)}, u32[]{:S(2)}, u32[]{:S(2)}) collective-permute-start(f32[14,64,128]{2,1,0:T(8,128)S(1)} %get-tuple-element.64.own), channel_id=1, source_target_pairs={{0,1},{1,0},{2,3},{3,2},{4,5},{5,4},{6,7},{7,6},{8,9},{9,8},{10,11... | collective-permute-start | bytes 1376264 | tf_op jit(solution)/shard_map/ppermute | solution.py:560
  16.6 9.0 %copy-start.2 = (f32[4,1,28,64,64]{4,3,2,1,0:T(8,128)S(1)}, f32[4,1,28,64,64]{4,3,2,1,0:T(8,128)}, u32[]{:S(2)}) copy-start(f32[4,1,28,64,64]{4,3,2,1,0:T(8,128)} %coarse.1) | copy-start | bytes 5505028
  18.6 26.6 %collective-permute-start.8 = (f32[22,64,128]{2,1,0:T(8,128)S(1)}, f32[22,64,128]{2,1,0:T(8,128)S(1)}, u32[]{:S(2)}, u32[]{:S(2)}) collective-permute-start(f32[22,64,128]{2,1,0:T(8,128)S(1)} %shard_map.55), channel_id=1, source_target_pairs={{1,2},{2,1},{3,4},{4,3},{5,6},{6,5},{7,8},{8,7},{9,10},{10,9},{11,... | collective-permute-start | bytes 2162696 | tf_op jit(solution)/shard_map/ppermute | solution.py:566
  19.4 11.9 %collective-permute-start.2 = (f32[14,64,128]{2,1,0:T(8,128)S(1)}, f32[14,64,128]{2,1,0:T(8,128)S(1)}, u32[]{:S(2)}, u32[]{:S(2)}) collective-permute-start(f32[14,64,128]{2,1,0:T(8,128)S(1)} %get-tuple-element.57), channel_id=1, source_target_pairs={{0,1},{1,0},{2,3},{3,2},{4,5},{5,4},{6,7},{7,6},{8,9},{9,8},{10,11... | collective-permute-start | bytes 1376264 | tf_op jit(solution)/shard_map/ppermute | solution.py:560
  25.0 6.3 %collective-permute-start.3 = (f32[14,64,128]{2,1,0:T(8,128)S(1)}, f32[14,64,128]{2,1,0:T(8,128)S(1)}, u32[]{:S(2)}, u32[]{:S(2)}) collective-permute-start(f32[14,64,128]{2,1,0:T(8,128)S(1)} %get-tuple-element.58), channel_id=1, source_target_pairs={{1,2},{2,1},{3,4},{4,3},{5,6},{6,5},{7,8},{8,7},{9,10},{10,9},{11,... | collective-permute-start | bytes 1376264 | tf_op jit(solution)/shard_map/ppermute | solution.py:566
  37.7 8.5 %collective-permute-start.4 = (f32[4,64,128]{2,1,0:T(8,128)S(1)}, f32[4,64,128]{2,1,0:T(8,128)S(1)}, u32[]{:S(2)}, u32[]{:S(2)}) collective-permute-start(f32[4,64,128]{2,1,0:T(8,128)S(1)} %get-tuple-element.63.own), channel_id=1, source_target_pairs={{0,1},{1,0},{2,3},{3,2},{4,5},{5,4},{6,7},{7,6},{8,9},{9,8},{10,11... | collective-permute-start | bytes 393224 | tf_op jit(solution)/shard_map/ppermute | solution.py:560
  45.2 9.1 %collective-permute-start.9 = (f32[22,64,128]{2,1,0:T(8,128)S(1)}, f32[22,64,128]{2,1,0:T(8,128)S(1)}, u32[]{:S(2)}, u32[]{:S(2)}) collective-permute-start(f32[22,64,128]{2,1,0:T(8,128)S(1)} %collective-permute-done.8.mine), channel_id=1, source_target_pairs={{0,1},{1,0},{2,3},{3,2},{4,5},{5,4},{6,7},{7,6},{8,9},{9,8},{10,11... | collective-permute-start | bytes 2162696 | tf_op jit(solution)/shard_map/ppermute | solution.py:560
  46.2 0.7 collective-permute-start.5
  46.9 8.5 %collective-permute-start.6 = (f32[8,64,128]{2,1,0:T(8,128)S(1)}, f32[8,64,128]{2,1,0:T(8,128)S(1)}, u32[]{:S(2)}, u32[]{:S(2)}) collective-permute-start(f32[8,64,128]{2,1,0:T(8,128)S(1)} %collective-permute-done.5.mine), channel_id=1, source_target_pairs={{0,1},{1,0},{2,3},{3,2},{4,5},{5,4},{6,7},{7,6},{8,9},{9,8},{10,11... | collective-permute-start | bytes 786440 | tf_op jit(solution)/shard_map/ppermute | solution.py:560
  57.3 14.5 %collective-permute-start.12 = (f32[2,64,128]{2,1,0:T(8,128)S(1)}, f32[2,64,128]{2,1,0:T(8,128)S(1)}, u32[]{:S(2)}, u32[]{:S(2)}) collective-permute-start(f32[2,64,128]{2,1,0:T(8,128)S(1)} %get-tuple-element.66.own), channel_id=1, source_target_pairs={{0,6},{1,7},{2,0},{3,1},{4,2},{5,3},{6,4},{7,5},{8,14},{9,15},{10,... | collective-permute-start | bytes 196616 | tf_op jit(solution)/shard_map/ppermute | solution.py:583
  66.4 6.0 %collective-permute-start.10 = (f32[2,64,128]{2,1,0:T(8,128)S(1)}, f32[2,64,128]{2,1,0:T(8,128)S(1)}, u32[]{:S(2)}, u32[]{:S(2)}) collective-permute-start(f32[2,64,128]{2,1,0:T(8,128)S(1)} %get-tuple-element.66.own), channel_id=1, source_target_pairs={{0,2},{1,3},{2,4},{3,5},{4,6},{5,7},{6,0},{7,1},{8,10},{9,11},{10,... | collective-permute-start | bytes 196616 | tf_op jit(solution)/shard_map/ppermute | solution.py:583
  66.4 5.4 %collective-permute-start.11 = (f32[1,64,128]{2,1,0:T(8,128)S(1)}, f32[1,64,128]{2,1,0:T(8,128)S(1)}, u32[]{:S(2)}, u32[]{:S(2)}) collective-permute-start(f32[1,64,128]{2,1,0:T(8,128)S(1)} %get-tuple-element.67), channel_id=1, source_target_pairs={{0,4},{1,5},{2,6},{3,7},{4,0},{5,1},{6,2},{7,3},{8,12},{9,13},{10,... | collective-permute-start | bytes 98312 | tf_op jit(solution)/shard_map/ppermute | solution.py:583
  72.5 11.6 %collective-permute-start.15 = (f32[5,64,128]{2,1,0:T(8,128)S(1)}, f32[5,64,128]{2,1,0:T(8,128)S(1)}, u32[]{:S(2)}, u32[]{:S(2)}) collective-permute-start(f32[5,64,128]{2,1,0:T(8,128)S(1)} %get-tuple-element.68.refs_0_), channel_id=1, source_target_pairs={{0,24},{1,25},{2,26},{3,27},{4,28},{5,29},{6,30},{7,31},{8,0},{9,1... | collective-permute-start | bytes 491528 | tf_op jit(solution)/shard_map/ppermute | solution.py:583
  74.8 9.3 %collective-permute-start.13 = (f32[5,64,128]{2,1,0:T(8,128)S(1)}, f32[5,64,128]{2,1,0:T(8,128)S(1)}, u32[]{:S(2)}, u32[]{:S(2)}) collective-permute-start(f32[5,64,128]{2,1,0:T(8,128)S(1)} %get-tuple-element.68.refs_0_), channel_id=1, source_target_pairs={{0,8},{1,9},{2,10},{3,11},{4,12},{5,13},{6,14},{7,15},{8,16},{9,17... | collective-permute-start | bytes 491528 | tf_op jit(solution)/shard_map/ppermute | solution.py:583
  74.8 9.2 %collective-permute-start.14 = (f32[4,64,128]{2,1,0:T(8,128)S(1)}, f32[4,64,128]{2,1,0:T(8,128)S(1)}, u32[]{:S(2)}, u32[]{:S(2)}) collective-permute-start(f32[4,64,128]{2,1,0:T(8,128)S(1)} %get-tuple-element.69), channel_id=1, source_target_pairs={{0,16},{1,17},{2,18},{3,19},{4,20},{5,21},{6,22},{7,23},{8,24},{9,... | collective-permute-start | bytes 393224 | tf_op jit(solution)/shard_map/ppermute | solution.py:583
  93.1 1.8 %collective-permute-start.16 = (f32[11,64,128]{2,1,0:T(8,128)S(1)}, f32[11,64,128]{2,1,0:T(8,128)S(1)}, u32[]{:S(2)}, u32[]{:S(2)}) collective-permute-start(f32[11,64,128]{2,1,0:T(8,128)S(1)} %get-tuple-element.83), channel_id=1, source_target_pairs={{0,1},{1,0},{2,3},{3,2},{4,5},{5,4},{6,7},{7,6},{8,9},{9,8},{10,11... | collective-permute-start | bytes 1081352 | tf_op jit(solution)/shard_map/ppermute | solution.py:560
  93.2 1.7 %collective-permute-start.17 = (f32[11,64,128]{2,1,0:T(8,128)S(1)}, f32[11,64,128]{2,1,0:T(8,128)S(1)}, u32[]{:S(2)}, u32[]{:S(2)}) collective-permute-start(f32[11,64,128]{2,1,0:T(8,128)S(1)} %get-tuple-element.84), channel_id=1, source_target_pairs={{1,2},{2,1},{3,4},{4,3},{5,6},{6,5},{7,8},{8,7},{9,10},{10,9},{11,... | collective-permute-start | bytes 1081352 | tf_op jit(solution)/shard_map/ppermute | solution.py:566
  99.9 8.6 %collective-permute-start.18 = (f32[4,64,128]{2,1,0:T(8,128)S(1)}, f32[4,64,128]{2,1,0:T(8,128)S(1)}, u32[]{:S(2)}, u32[]{:S(2)}) collective-permute-start(f32[4,64,128]{2,1,0:T(8,128)S(1)} %get-tuple-element.86.own), channel_id=1, source_target_pairs={{0,1},{1,0},{2,3},{3,2},{4,5},{5,4},{6,7},{7,6},{8,9},{9,8},{10,11... | collective-permute-start | bytes 393224 | tf_op jit(solution)/shard_map/ppermute | solution.py:560
  108.6 32.9 %copy-start.3 = (s32[1,32]{1,0:T(1,128)S(1)}, s32[1,32]{1,0:T(1,128)}, u32[]{:S(2)}) copy-start(s32[1,32]{1,0:T(1,128)} %refs_0_.1) | copy-start | bytes 388
  108.6 0.7 collective-permute-start.19
  109.3 8.5 %collective-permute-start.20 = (f32[8,64,128]{2,1,0:T(8,128)S(1)}, f32[8,64,128]{2,1,0:T(8,128)S(1)}, u32[]{:S(2)}, u32[]{:S(2)}) collective-permute-start(f32[8,64,128]{2,1,0:T(8,128)S(1)} %collective-permute-done.19.mine), channel_id=1, source_target_pairs={{0,1},{1,0},{2,3},{3,2},{4,5},{5,4},{6,7},{7,6},{8,9},{9,8},{10,11... | collective-permute-start | bytes 786440 | tf_op jit(solution)/shard_map/ppermute | solution.py:560
  119.7 11.3 %collective-permute-start.23 = (f32[2,64,128]{2,1,0:T(8,128)S(1)}, f32[2,64,128]{2,1,0:T(8,128)S(1)}, u32[]{:S(2)}, u32[]{:S(2)}) collective-permute-start(f32[2,64,128]{2,1,0:T(8,128)S(1)} %get-tuple-element.87.own), channel_id=1, source_target_pairs={{0,6},{1,7},{2,0},{3,1},{4,2},{5,3},{6,4},{7,5},{8,14},{9,15},{10,... | collective-permute-start | bytes 196616 | tf_op jit(solution)/shard_map/ppermute | solution.py:583
  125.6 6.0 %collective-permute-start.21 = (f32[2,64,128]{2,1,0:T(8,128)S(1)}, f32[2,64,128]{2,1,0:T(8,128)S(1)}, u32[]{:S(2)}, u32[]{:S(2)}) collective-permute-start(f32[2,64,128]{2,1,0:T(8,128)S(1)} %get-tuple-element.87.own), channel_id=1, source_target_pairs={{0,2},{1,3},{2,4},{3,5},{4,6},{5,7},{6,0},{7,1},{8,10},{9,11},{10,... | collective-permute-start | bytes 196616 | tf_op jit(solution)/shard_map/ppermute | solution.py:583
  125.6 5.4 %collective-permute-start.22 = (f32[1,64,128]{2,1,0:T(8,128)S(1)}, f32[1,64,128]{2,1,0:T(8,128)S(1)}, u32[]{:S(2)}, u32[]{:S(2)}) collective-permute-start(f32[1,64,128]{2,1,0:T(8,128)S(1)} %get-tuple-element.88), channel_id=1, source_target_pairs={{0,4},{1,5},{2,6},{3,7},{4,0},{5,1},{6,2},{7,3},{8,12},{9,13},{10,... | collective-permute-start | bytes 98312 | tf_op jit(solution)/shard_map/ppermute | solution.py:583
  131.6 9.7 %collective-permute-start.26 = (f32[5,64,128]{2,1,0:T(8,128)S(1)}, f32[5,64,128]{2,1,0:T(8,128)S(1)}, u32[]{:S(2)}, u32[]{:S(2)}) collective-permute-start(f32[5,64,128]{2,1,0:T(8,128)S(1)} %get-tuple-element.89.refs_1_), channel_id=1, source_target_pairs={{0,24},{1,25},{2,26},{3,27},{4,28},{5,29},{6,30},{7,31},{8,0},{9,1... | collective-permute-start | bytes 491528 | tf_op jit(solution)/shard_map/ppermute | solution.py:583
  131.8 9.6 %collective-permute-start.24 = (f32[5,64,128]{2,1,0:T(8,128)S(1)}, f32[5,64,128]{2,1,0:T(8,128)S(1)}, u32[]{:S(2)}, u32[]{:S(2)}) collective-permute-start(f32[5,64,128]{2,1,0:T(8,128)S(1)} %get-tuple-element.89.refs_1_), channel_id=1, source_target_pairs={{0,8},{1,9},{2,10},{3,11},{4,12},{5,13},{6,14},{7,15},{8,16},{9,17... | collective-permute-start | bytes 491528 | tf_op jit(solution)/shard_map/ppermute | solution.py:583
  133.7 7.6 %collective-permute-start.25 = (f32[4,64,128]{2,1,0:T(8,128)S(1)}, f32[4,64,128]{2,1,0:T(8,128)S(1)}, u32[]{:S(2)}, u32[]{:S(2)}) collective-permute-start(f32[4,64,128]{2,1,0:T(8,128)S(1)} %get-tuple-element.90), channel_id=1, source_target_pairs={{0,16},{1,17},{2,18},{3,19},{4,20},{5,21},{6,22},{7,23},{8,24},{9,... | collective-permute-start | bytes 393224 | tf_op jit(solution)/shard_map/ppermute | solution.py:583
  149.7 10.4 %collective-permute-start.27 = (f32[8,64,128]{2,1,0:T(8,128)S(1)}, f32[8,64,128]{2,1,0:T(8,128)S(1)}, u32[]{:S(2)}, u32[]{:S(2)}) collective-permute-start(f32[8,64,128]{2,1,0:T(8,128)S(1)} %get-tuple-element.104), channel_id=1, source_target_pairs={{0,32},{32,64},{64,96},{96,0},{1,33},{33,65},{65,97},{97,1},{2,34}... | collective-permute-start | bytes 786440 | tf_op jit(solution)/shard_map/ppermute | solution.py:670
  151.7 13.4 %collective-permute-start.28 = (f32[8,64,128]{2,1,0:T(8,128)S(1)}, f32[8,64,128]{2,1,0:T(8,128)S(1)}, u32[]{:S(2)}, u32[]{:S(2)}) collective-permute-start(f32[8,64,128]{2,1,0:T(8,128)S(1)} %get-tuple-element.105), channel_id=1, source_target_pairs={{0,64},{32,96},{64,0},{96,32},{1,65},{33,97},{65,1},{97,33},{2,66}... | collective-permute-start | bytes 786440 | tf_op jit(solution)/shard_map/ppermute | solution.py:670
  155.3 9.8 %collective-permute-start.29 = (f32[8,64,128]{2,1,0:T(8,128)S(1)}, f32[8,64,128]{2,1,0:T(8,128)S(1)}, u32[]{:S(2)}, u32[]{:S(2)}) collective-permute-start(f32[8,64,128]{2,1,0:T(8,128)S(1)} %get-tuple-element.106), channel_id=1, source_target_pairs={{0,96},{32,0},{64,32},{96,64},{1,97},{33,1},{65,33},{97,65},{2,98}... | collective-permute-start | bytes 786440 | tf_op jit(solution)/shard_map/ppermute | solution.py:670
  (2 other events, 5.5 us)
where the time goes:
time: 167 us; the launch traced here: 166 us
  starting transfers between devices  76.2 us (46%)
  Pallas kernels  53.2 us (32%)
  waiting for transfers between devices  34.9 us (21%)
    ppermute x9, starting transfers between devices, swap_in(): return lax.ppermute(value, 'dev', [(i, i ^ 1) for i in range(devices)])  38.8 us
    ppermute x12, starting transfers between devices, shift(): return lax.ppermute(value, 'dev', route)  26.8 us
    ppermute x12, waiting for transfers between devices, shift(): return lax.ppermute(value, 'dev', route)  21.7 us
    pallas_call x2, Pallas kernels, cycle(): call(functools.partial(up_kernel, last), ([SMEM] if last else []) + [VMEM...  17.2 us
    ppermute x3, waiting for transfers between devices, shards(): lax.ppermute(parts[s], 'grp', [(i, (i + s) % groups) for i in range(group...  8.79 us
    ppermute x3, starting transfers between devices, shards(): lax.ppermute(parts[s], 'grp', [(i, (i + s) % groups) for i in range(group...  6.58 us
    pallas_call x2, Pallas kernels, cycle(): call(functools.partial(down_fine_kernel, at), [VMEM] * 4, [shape(54, B, K...  6.22 us
    pallas_call x1, Pallas kernels, shards(): call(own_rest_kernel, [ANY, ANY], [split_shape(26), split_shape(12), spli...  5.6 us
  transfers between devices with their start and end apart: 30, of which 14 were waited for; matrix products, arithmetic and copies ran while one was open for 0% of the time, Pallas kernels for 13%

commit v1 on v0

--- a/solution.py
+++ b/solution.py
@@ -61,7 +61,7 @@
     return carry
 
 
-def smooth(rows, q_ref, q_at, source, store, size=12):
+def smooth(rows, q_ref, q_at, source, store, size=17):
     def body(first, count, carry):
         values = [source(first + u) for u in range(count)]
         outs = [product(q_ref[q_at + first + u, 0:64, :], values[u]) for u in range(count)]
@@ -72,7 +72,7 @@
     grouped(0, rows, size, body)
 
 
-def sweep(rows, q_ref, q_at, source, emit, size=13):
+def sweep(rows, q_ref, q_at, source, emit, size=17):
     def lower(k):
         return q_ref[q_at + k, 64:128, :]
 
@@ -218,29 +218,20 @@
     lax.fori_loop(0, rows // 2, pair_of_rows, 0)
 
 
-def own_kernel(ops, q0, buf, sems):
+def own_kernel(ops, q0, q1, q2, buf, sems):
     copies = Copies(sems)
     parts = []
-    for begin in (0, 16):
-        part = pl.ds(begin, 16)
-        parts.append(copies.start(ops.at[:, part], buf.at[:, part]))
-    for begin, part in zip((0, 16), parts):
-        part.wait()
-        split_rows(buf, begin, 16, q0, HALO[0] + begin)
-
-
-def own_rest_kernel(ops, coarse, q1, q2, qc, buf, cbuf, sems):
-    copies = Copies(sems)
-    loads = [
-        copies.start(ops.at[:, pl.ds(32, 24)], buf),
-        copies.start(coarse.at[:, 0], cbuf),
-    ]
-    loads[0].wait()
-    split_rows(buf, 0, 16, q1, HALO[1])
-    split_rows(buf, 16, 8, q2, HALO[2])
-    loads[1].wait()
+    for begin, rows, target, at in ((0, 16, q0, 11), (16, 16, q0, 27), (32, 16, q1, 5), (48, 8, q2, 2)):
+        part = pl.ds(begin, rows)
+        parts.append((copies.start(ops.at[:, part], buf.at[:, part]), begin, rows, target, at))
+    for load, begin, rows, target, at in parts:
+        load.wait()
+        split_rows(buf, begin, rows, target, at)
+
+
+def own_coarse_kernel(coarse, qc):
     for level in range(3):
-        split_rows(cbuf, COARSE_AT[level], COARSE[level], qc, COARSE_IN[level])
+        split_rows(coarse, COARSE_AT[level], COARSE[level], qc, COARSE_IN[level])
 
 
 def halo_kernel(levels, got_in, got_out, *refs):
@@ -567,7 +558,8 @@
 
     def around(value):
         partner = swap_in(value)
-        mine = swap_out(jnp.concatenate([value, partner], axis=0))
+        both = jnp.concatenate([value, partner], axis=0)
+        mine = swap_out(both)
         theirs = swap_in(mine)
         return value, partner, mine, theirs
 
@@ -583,11 +575,13 @@
         return lax.ppermute(value, "dev", route)
 
     def gather(c6, c6_x5):
-        parts = (c6_x5, shift(c6_x5, False, 1), shift(c6, False, 2), shift(c6_x5, False, 3))
+        across = shift(c6, False, 2)
+        parts = (c6_x5, shift(c6_x5, False, 1), across, shift(c6_x5, False, 3))
         row, row_x5 = call(
             row_kernel, [VMEM] * 4, [shape(4, B, K), shape(5, B, K)], size=1 << 18
         )(*parts)
-        return [row_x5, shift(row_x5, True, 1), shift(row, True, 2), shift(row_x5, True, 3)]
+        across = shift(row, True, 2)
+        return [row_x5, shift(row_x5, True, 1), across, shift(row_x5, True, 3)]
 
     halo = HALO[0]
 
@@ -597,23 +591,21 @@
             [pltpu.VMEM((4, halo, B, B), F32), pltpu.SemaphoreType.DMA((3,))], size=4 << 20, room=58,
         )(local_ops, adjoint_load)
 
-    got_out = swap_out(send(True))
-    got_in = swap_in(send(False))
+    to_out = send(True)
+    got_out = swap_out(to_out)
+    to_in = send(False)
+    got_in = swap_in(to_in)
     rest_in, rest_out, own7 = call(
         send_rest_kernel, [ANY], [shape(14, B, K)] * 3,
         [pltpu.VMEM((4, 21, B, B), F32), pltpu.SemaphoreType.DMA((5,))], size=4 << 20, room=50,
     )(local_ops)
     more_out = swap_out(rest_out)
     more_in = swap_in(rest_in)
-    q0 = call(
-        own_kernel, [ANY], [split_shape(54)],
-        [pltpu.VMEM((4, 32, B, B), F32), pltpu.SemaphoreType.DMA((2,))], size=8 << 20, room=40,
-    )(local_ops)[0]
-    q1, q2, qc = call(
-        own_rest_kernel, [ANY, ANY], [split_shape(26), split_shape(12), split_shape(34)],
-        [pltpu.VMEM((4, 24, B, B), F32), pltpu.VMEM((4, 28, B, B), F32), pltpu.SemaphoreType.DMA((2,))],
-        size=12 << 20, room=24,
-    )(local_ops, coarse_ops)
+    q0, q1, q2 = call(
+        own_kernel, [ANY], [split_shape(54), split_shape(26), split_shape(12)],
+        [pltpu.VMEM((4, 56, B, B), F32), pltpu.SemaphoreType.DMA((4,))], size=8 << 20, room=40,
+    )(local_ops)
+    qc = call(own_coarse_kernel, [VMEM], split_shape(34), size=6 << 20)(coarse_ops[:, 0])
     q0 = call(
         functools.partial(halo_kernel, (0,)), [VMEM] * 3, [split_shape(54)],
         size=4 << 20, aliases={2: 0},
@@ -626,9 +618,10 @@
     both = call(chip_send_kernel, [VMEM] * 2, shape(22, B, K), size=2 << 20)(own7, partner7)
     both = lax.optimization_barrier((both, q0))[0]
     mine = swap_out(both)
+    theirs = swap_in(mine)
     q_chip = call(
         chip_kernel, [VMEM] * 4, split_shape(CHIPQ_ROWS), size=6 << 20,
-    )(own7, partner7, mine, swap_in(mine))
+    )(own7, partner7, mine, theirs)
 
     def cycle(at, load, load_in, load_out, earlier=None):
         last = earlier is not None

time: 167 us -> 164 us (0.982)
  Pallas kernels: 53.2 us -> 50.2 us
  starting transfers between devices: 76.2 us -> 78.7 us
  waiting for transfers between devices: 34.9 us -> 32.9 us
    ppermute x12, waiting for transfers between devices: 21.7 us -> 19 us  [shift(): return lax.ppermute(value, 'dev', route)]
    ppermute x9, starting transfers between devices: 38.8 us -> 41.1 us  [swap_in(): return lax.ppermute(value, 'dev', [(i, i ^ 1) for i in range(devices)])]
  transfers between devices with their start and end apart: 30 -> 30, of which waited for: 14 -> 15; matrix products, arithmetic and copies ran while one was open for 0% -> 0% of each run, Pallas kernels for 13% -> 13%
where the time goes in v1:
time: 164 us
  starting transfers between devices  78.7 us (48%)
  Pallas kernels  50.2 us (31%)
  waiting for transfers between devices  32.9 us (20%)
    ppermute x9, starting transfers between devices, swap_in(): return lax.ppermute(value, 'dev', [(i, i ^ 1) for i in range(devices)])  41.1 us
    ppermute x12, starting transfers between devices, shift(): return lax.ppermute(value, 'dev', route)  26.8 us
    ppermute x12, waiting for transfers between devices, shift(): return lax.ppermute(value, 'dev', route)  19 us
    pallas_call x2, Pallas kernels, cycle(): call(functools.partial(up_kernel, last), ([SMEM] if last else []) + [VMEM...  15.7 us
    ppermute x3, waiting for transfers between devices, shards(): lax.ppermute(parts[s], 'grp', [(i, (i + s) % groups) for i in range(group...  8.81 us
    ppermute x3, starting transfers between devices, shards(): lax.ppermute(parts[s], 'grp', [(i, (i + s) % groups) for i in range(group...  6.56 us
    pallas_call x1, Pallas kernels, shards(): call(own_kernel, [ANY], [split_shape(54), split_shape(26), split_shape(12...  6.05 us
    pallas_call x2, Pallas kernels, cycle(): call(functools.partial(down_fine_kernel, at), [VMEM] * 4, [shape(54, B, K...  5.53 us
  transfers between devices with their start and end apart: 30, of which 15 were waited for; matrix products, arithmetic and copies ran while one was open for 0% of the time, Pallas kernels for 13%

profile of v1, /device:TPU:0, one launch (start us, length us, event | category | flops | bytes accessed | tf_op | source)
XLA Modules:
  0.0 163.6 jit_solution(6029780786068789665)
XLA Ops:
  0.0 2.5 %shard_map.47 = f32[33,64,128]{2,1,0:T(8,128)} custom-call(f32[4,63,64,64]{3,2,1,0:T(8,128)} %ops.7, f32[32,64,128]{2,1,0:T(8,128)} %load.5), custom_call_target="tpu_custom_call" | custom-call | bytes 4194304 | tf_op jit(solution)/shard_map/pallas_call | solution.py:589
  3.3 2.5 %shard_map.46 = f32[33,64,128]{2,1,0:T(8,128)} custom-call(f32[4,63,64,64]{3,2,1,0:T(8,128)} %ops.7, f32[32,64,128]{2,1,0:T(8,128)} %load.5), custom_call_target="tpu_custom_call" | custom-call | bytes 4194304 | tf_op jit(solution)/shard_map/pallas_call | solution.py:589
  5.8 3.0 %collective-permute-start = (f32[33,64,128]{2,1,0:T(8,128)}, f32[33,64,128]{2,1,0:T(8,128)S(1)}, u32[]{:S(2)}, u32[]{:S(2)}) collective-permute-start(f32[33,64,128]{2,1,0:T(8,128)} %shard_map.46), channel_id=1, source_target_pairs={{0,1},{1,0},{2,3},{3,2},{4,5},{5,4},{6,7},{7,6},{8,9},{9,8},{10,11... | collective-permute-start | bytes 3244040 | tf_op jit(solution)/shard_map/ppermute | solution.py:551
  8.8 2.7 %shard_map.51 = (f32[14,64,128]{2,1,0:T(8,128)S(1)}, f32[14,64,128]{2,1,0:T(8,128)S(1)}, f32[14,64,128]{2,1,0:T(8,128)S(1)}) custom-call(f32[4,63,64,64]{3,2,1,0:T(8,128)} %ops.7), custom_call_target="tpu_custom_call" | custom-call | bytes 4194304 | tf_op jit(solution)/shard_map/pallas_call | solution.py:598
  13.0 6.1 %shard_map.48 = (bf16[54,256,128]{2,1,0:T(8,128)(2,1)S(1)}, bf16[26,256,128]{2,1,0:T(8,128)(2,1)S(1)}, bf16[12,256,128]{2,1,0:T(8,128)(2,1)S(1)}) custom-call(f32[4,63,64,64]{3,2,1,0:T(8,128)S(1)} %copy-done), custom_call_target="tpu_custom_call" | custom-call | bytes 8388608 | tf_op jit(solution)/shard_map/pallas_call | solution.py:604
  19.2 2.0 %shard_map.49.q0.refs_20_.refs_21_ = bf16[54,256,128]{2,1,0:T(8,128)(2,1)S(1)} custom-call(f32[33,64,128]{2,1,0:T(8,128)S(1)} %collective-permute-done.got_in.load_in, f32[33,64,128]{2,1,0:T(8,128)S(1)} %collective-permute-done.1.got_out.load_out, bf16[54,256,128]{2,1,0:T(8,128)(2,1)S(1)} %get-tuple-element.56.refs_0_), custom_call_target="tpu_custom_call", output_to_operand_aliasing={{}: (2, {})} | custom-call | bytes 4194304 | tf_op jit(solution)/shard_map/pallas_call | solution.py:609
  22.1 3.0 %collective-permute-start.2 = (f32[14,64,128]{2,1,0:T(8,128)S(1)}, f32[14,64,128]{2,1,0:T(8,128)S(1)}, u32[]{:S(2)}, u32[]{:S(2)}) collective-permute-start(f32[14,64,128]{2,1,0:T(8,128)S(1)} %get-tuple-element.58), channel_id=1, source_target_pairs={{0,1},{1,0},{2,3},{3,2},{4,5},{5,4},{6,7},{7,6},{8,9},{9,8},{10,11... | collective-permute-start | bytes 1376264 | tf_op jit(solution)/shard_map/ppermute | solution.py:551
  27.8 2.8 %shard_map.50 = (f32[54,64,128]{2,1,0:T(8,128)S(1)}, f32[54,64,128]{2,1,0:T(8,128)S(1)}, f32[26,64,128]{2,1,0:T(8,128)S(1)}) custom-call(f32[32,64,128]{2,1,0:T(8,128)S(1)} %copy-done.1, f32[33,64,128]{2,1,0:T(8,128)S(1)} %collective-permute-done.got_in.load_in, f32[33,64,128]{2,1,0:T(8,128)S(1)} %collective-permute-done.1.got_out.load_out, ...), custom_call_target="tpu_custom_call" | custom-call | flops 905969664 | bytes 16777216 | tf_op jit(solution)/shard_map/pallas_call | solution.py:628
  32.3 12.4 %collective-permute-start.4 = (f32[4,64,128]{2,1,0:T(8,128)S(1)}, f32[4,64,128]{2,1,0:T(8,128)S(1)}, u32[]{:S(2)}, u32[]{:S(2)}) collective-permute-start(f32[4,64,128]{2,1,0:T(8,128)S(1)} %get-tuple-element.64.own), channel_id=1, source_target_pairs={{0,1},{1,0},{2,3},{3,2},{4,5},{5,4},{6,7},{7,6},{8,9},{9,8},{10,11... | collective-permute-start | bytes 393224 | tf_op jit(solution)/shard_map/ppermute | solution.py:551
  46.4 7.4 %collective-permute-start.6 = (f32[8,64,128]{2,1,0:T(8,128)S(1)}, f32[8,64,128]{2,1,0:T(8,128)S(1)}, u32[]{:S(2)}, u32[]{:S(2)}) collective-permute-start(f32[8,64,128]{2,1,0:T(8,128)S(1)} %collective-permute-done.5.mine), channel_id=1, source_target_pairs={{0,1},{1,0},{2,3},{3,2},{4,5},{5,4},{6,7},{7,6},{8,9},{9,8},{10,11... | collective-permute-start | bytes 786440 | tf_op jit(solution)/shard_map/ppermute | solution.py:551
  55.0 1.9 %shard_map.56 = (f32[1,64,128]{2,1,0:T(8,128)S(1)}, f32[2,64,128]{2,1,0:T(8,128)S(1)}, f32[22,64,128]{2,1,0:T(8,128)S(1)}, f32[24,64,128]{2,1,0:T(8,128)S(1)}, f...) custom-call(f32[4,64,128]{2,1,0:T(8,128)S(1)} %get-tuple-element.64., ...), custom_call_target="tpu_custom_call" | custom-call | flops 603979776 | bytes 6291456 | tf_op jit(solution)/shard_map/pallas_call | solution.py:638
  56.8 9.1 %collective-permute-start.12 = (f32[2,64,128]{2,1,0:T(8,128)S(1)}, f32[2,64,128]{2,1,0:T(8,128)S(1)}, u32[]{:S(2)}, u32[]{:S(2)}) collective-permute-start(f32[2,64,128]{2,1,0:T(8,128)S(1)} %get-tuple-element.67.own), channel_id=1, source_target_pairs={{0,6},{1,7},{2,0},{3,1},{4,2},{5,3},{6,4},{7,5},{8,14},{9,15},{10,... | collective-permute-start | bytes 196616 | tf_op jit(solution)/shard_map/ppermute | solution.py:575
  67.5 3.9 %collective-permute-done.11.across = f32[1,64,128]{2,1,0:T(8,128)S(1)} collective-permute-done((f32[1,64,128]{2,1,0:T(8,128)S(1)}, f32[1,64,128]{2,1,0:T(8,128)S(1)}, u32[]{:S(2)}, u32[]{:S(2)}) %collective-permute-start.11) | collective-permute-done | bytes 32800 | tf_op jit(solution)/shard_map/ppermute | solution.py:575
  72.0 2.3 %collective-permute-start.15 = (f32[5,64,128]{2,1,0:T(8,128)S(1)}, f32[5,64,128]{2,1,0:T(8,128)S(1)}, u32[]{:S(2)}, u32[]{:S(2)}) collective-permute-start(f32[5,64,128]{2,1,0:T(8,128)S(1)} %get-tuple-element.69.refs_0_), channel_id=1, source_target_pairs={{0,24},{1,25},{2,26},{3,27},{4,28},{5,29},{6,30},{7,31},{8,0},{9,1... | collective-permute-start | bytes 491528 | tf_op jit(solution)/shard_map/ppermute | solution.py:575
  74.3 3.0 %collective-permute-start.14 = (f32[4,64,128]{2,1,0:T(8,128)S(1)}, f32[4,64,128]{2,1,0:T(8,128)S(1)}, u32[]{:S(2)}, u32[]{:S(2)}) collective-permute-start(f32[4,64,128]{2,1,0:T(8,128)S(1)} %get-tuple-element.70), channel_id=1, source_target_pairs={{0,16},{1,17},{2,18},{3,19},{4,20},{5,21},{6,22},{7,23},{8,24},{9,... | collective-permute-start | bytes 393224 | tf_op jit(solution)/shard_map/ppermute | solution.py:575
  77.3 2.8 %shard_map.58.refs_16_.refs_17_ = bf16[34,256,128]{2,1,0:T(8,128)(2,1)S(1)} custom-call(f32[4,28,64,64]{3,2,1,0:T(8,128)S(1)} %bitcast.1), custom_call_target="tpu_custom_call" | custom-call | bytes 6291456 | tf_op jit(solution)/shard_map/pallas_call | solution.py:608
  80.0 3.5 %collective-permute-done.14.refs_2_ = f32[4,64,128]{2,1,0:T(8,128)S(1)} collective-permute-done((f32[4,64,128]{2,1,0:T(8,128)S(1)}, f32[4,64,128]{2,1,0:T(8,128)S(1)}, u32[]{:S(2)}, u32[]{:S(2)}) %collective-permute-start.14) | collective-permute-done | bytes 131104 | tf_op jit(solution)/shard_map/ppermute | solution.py:575
  83.6 8.0 %shard_map.59 = (f32[32,64,128]{2,1,0:T(8,128)S(1)}, f32[32,64,128]{2,1,0:T(8,128)S(1)}, f32[11,64,128]{2,1,0:T(8,128)S(1)}, f32[11,64,128]{2,1,0:T(8,128)S(1)}) custom-call(f32[5,64,128]{2,1,0:T(8,128)S(1)} %get-tuple-element.69.refs_0_, f32[5,64,128]{2,1,0:T(8,128)S(1)} %collective-permute-done.13.refs_1_, ...), custom_call_target="tpu_custom_call" | custom-call | flops 2181038080 | bytes 20971520 | tf_op jit(solution)/shard_map/pallas_call | solution.py:648
  93.4 2.8 %shard_map.60 = (f32[54,64,128]{2,1,0:T(8,128)S(1)}, f32[54,64,128]{2,1,0:T(8,128)S(1)}, f32[26,64,128]{2,1,0:T(8,128)S(1)}) custom-call(f32[32,64,128]{2,1,0:T(8,128)S(1)} %get-tuple-element.82.load, f32[11,64,128]{2,1,0:T(8,128)S(1)} %collective-permute-done.16.load_in, f32[11,64,128]{2,1,0:T(8,128)S(1)} %collective-permute-done.17.load_out, ...), custom_call_target="tpu_custom_call" | custom-call | flops 905969664 | bytes 16777216 | tf_op jit(solution)/shard_map/pallas_call | solution.py:628
  96.2 1.7 %shard_map.61 = (f32[26,64,128]{2,1,0:T(8,128)S(1)}, f32[12,64,128]{2,1,0:T(8,128)S(1)}, f32[12,64,128]{2,1,0:T(8,128)S(1)}, f32[4,64,128]{2,1,0:T(8,128)S(1)}) custom-call(f32[26,64,128]{2,1,0:T(8,128)S(1)} %get-tuple-element.85.b1.refs_14_, bf16[26,256,128]{2,1,0:T(8,128)(2,1)S(1)} %get-tuple-element.62.q1.refs_19_.refs_20_, ...), custom_call_target="tpu_custom_call" | custom-call | flops 637534208 | bytes 8388608 | tf_op jit(solution)/shard_map/pallas_call | solution.py:633
  97.8 7.6 %collective-permute-start.18 = (f32[4,64,128]{2,1,0:T(8,128)S(1)}, f32[4,64,128]{2,1,0:T(8,128)S(1)}, u32[]{:S(2)}, u32[]{:S(2)}) collective-permute-start(f32[4,64,128]{2,1,0:T(8,128)S(1)} %get-tuple-element.86.own), channel_id=1, source_target_pairs={{0,1},{1,0},{2,3},{3,2},{4,5},{5,4},{6,7},{7,6},{8,9},{9,8},{10,11... | collective-permute-start | bytes 393224 | tf_op jit(solution)/shard_map/ppermute | solution.py:551
  107.2 7.4 %collective-permute-start.20 = (f32[8,64,128]{2,1,0:T(8,128)S(1)}, f32[8,64,128]{2,1,0:T(8,128)S(1)}, u32[]{:S(2)}, u32[]{:S(2)}) collective-permute-start(f32[8,64,128]{2,1,0:T(8,128)S(1)} %collective-permute-done.19.mine), channel_id=1, source_target_pairs={{0,1},{1,0},{2,3},{3,2},{4,5},{5,4},{6,7},{7,6},{8,9},{9,8},{10,11... | collective-permute-start | bytes 786440 | tf_op jit(solution)/shard_map/ppermute | solution.py:551
  115.7 1.9 %shard_map.62 = (f32[1,64,128]{2,1,0:T(8,128)S(1)}, f32[2,64,128]{2,1,0:T(8,128)S(1)}, f32[22,64,128]{2,1,0:T(8,128)S(1)}, f32[24,64,128]{2,1,0:T(8,128)S(1)}, f...) custom-call(f32[4,64,128]{2,1,0:T(8,128)S(1)} %get-tuple-element.86., ...), custom_call_target="tpu_custom_call" | custom-call | flops 603979776 | bytes 6291456 | tf_op jit(solution)/shard_map/pallas_call | solution.py:638
  117.6 5.9 %collective-permute-start.23 = (f32[2,64,128]{2,1,0:T(8,128)S(1)}, f32[2,64,128]{2,1,0:T(8,128)S(1)}, u32[]{:S(2)}, u32[]{:S(2)}) collective-permute-start(f32[2,64,128]{2,1,0:T(8,128)S(1)} %get-tuple-element.87.own), channel_id=1, source_target_pairs={{0,6},{1,7},{2,0},{3,1},{4,2},{5,3},{6,4},{7,5},{8,14},{9,15},{10,... | collective-permute-start | bytes 196616 | tf_op jit(solution)/shard_map/ppermute | solution.py:575
  125.0 3.9 %collective-permute-done.22.across = f32[1,64,128]{2,1,0:T(8,128)S(1)} collective-permute-done((f32[1,64,128]{2,1,0:T(8,128)S(1)}, f32[1,64,128]{2,1,0:T(8,128)S(1)}, u32[]{:S(2)}, u32[]{:S(2)}) %collective-permute-start.22) | collective-permute-done | bytes 32800 | tf_op jit(solution)/shard_map/ppermute | solution.py:575
  129.8 1.9 %collective-permute-start.24 = (f32[5,64,128]{2,1,0:T(8,128)S(1)}, f32[5,64,128]{2,1,0:T(8,128)S(1)}, u32[]{:S(2)}, u32[]{:S(2)}) collective-permute-start(f32[5,64,128]{2,1,0:T(8,128)S(1)} %get-tuple-element.89.refs_1_), channel_id=1, source_target_pairs={{0,8},{1,9},{2,10},{3,11},{4,12},{5,13},{6,14},{7,15},{8,16},{9,17... | collective-permute-start | bytes 491528 | tf_op jit(solution)/shard_map/ppermute | solution.py:575
  132.9 6.3 %collective-permute-done.25.refs_3_ = f32[4,64,128]{2,1,0:T(8,128)S(1)} collective-permute-done((f32[4,64,128]{2,1,0:T(8,128)S(1)}, f32[4,64,128]{2,1,0:T(8,128)S(1)}, u32[]{:S(2)}, u32[]{:S(2)}) %collective-permute-start.25) | collective-permute-done | bytes 131104 | tf_op jit(solution)/shard_map/ppermute | solution.py:575
  139.4 7.6 %shard_map.64 = (f32[8,64,128]{2,1,0:T(8,128)S(1)}, f32[8,64,128]{2,1,0:T(8,128)S(1)}, f32[8,64,128]{2,1,0:T(8,128)S(1)}, f32[8,64,128]{2,1,0:T(8,128)S(1)}) custom-call(s32[1,32]{1,0:T(1,128)S(1)} %copy-done.3, f32[5,64,128]{2,1,0:T(8,128)S(1)} %get-tuple-element.89.refs_1_, f32[5,64,128]{2,1,0:T(8,128)S(1)} %collective-permute-done.24.refs_2_, ...), custom_call_target="tpu_custom_call" | custom-call | flops 2181038080 | bytes 20971520 | tf_op jit(solution)/shard_map/pallas_call | solution.py:648
  147.0 2.0 %collective-permute-start.27 = (f32[8,64,128]{2,1,0:T(8,128)S(1)}, f32[8,64,128]{2,1,0:T(8,128)S(1)}, u32[]{:S(2)}, u32[]{:S(2)}) collective-permute-start(f32[8,64,128]{2,1,0:T(8,128)S(1)} %get-tuple-element.104), channel_id=1, source_target_pairs={{0,32},{32,64},{64,96},{96,0},{1,33},{33,65},{65,97},{97,1},{2,34}... | collective-permute-start | bytes 786440 | tf_op jit(solution)/shard_map/ppermute | solution.py:663
  149.0 3.6 %collective-permute-start.28 = (f32[8,64,128]{2,1,0:T(8,128)S(1)}, f32[8,64,128]{2,1,0:T(8,128)S(1)}, u32[]{:S(2)}, u32[]{:S(2)}) collective-permute-start(f32[8,64,128]{2,1,0:T(8,128)S(1)} %get-tuple-element.105), channel_id=1, source_target_pairs={{0,64},{32,96},{64,0},{96,32},{1,65},{33,97},{65,1},{97,33},{2,66}... | collective-permute-start | bytes 786440 | tf_op jit(solution)/shard_map/ppermute | solution.py:663
  153.6 3.8 %collective-permute-done.27.part1 = f32[8,64,128]{2,1,0:T(8,128)S(1)} collective-permute-done((f32[8,64,128]{2,1,0:T(8,128)S(1)}, f32[8,64,128]{2,1,0:T(8,128)S(1)}, u32[]{:S(2)}, u32[]{:S(2)}) %collective-permute-start.27) | collective-permute-done | bytes 262176 | tf_op jit(solution)/shard_map/ppermute | solution.py:663
  157.4 5.0 %collective-permute-done.28.part2 = f32[8,64,128]{2,1,0:T(8,128)S(1)} collective-permute-done((f32[8,64,128]{2,1,0:T(8,128)S(1)}, f32[8,64,128]{2,1,0:T(8,128)S(1)}, u32[]{:S(2)}, u32[]{:S(2)}) %collective-permute-start.28) | collective-permute-done | bytes 262176 | tf_op jit(solution)/shard_map/ppermute | solution.py:663
  (58 shorter events, 23.0 us)
Async XLA Ops:
  2.5 16.6 %collective-permute-start.1 = (f32[33,64,128]{2,1,0:T(8,128)}, f32[33,64,128]{2,1,0:T(8,128)S(1)}, u32[]{:S(2)}, u32[]{:S(2)}) collective-permute-start(f32[33,64,128]{2,1,0:T(8,128)} %shard_map.47), channel_id=1, source_target_pairs={{1,2},{2,1},{3,4},{4,3},{5,6},{6,5},{7,8},{8,7},{9,10},{10,9},{11,... | collective-permute-start | bytes 3244040 | tf_op jit(solution)/shard_map/ppermute | solution.py:557
  5.8 13.4 %collective-permute-start = (f32[33,64,128]{2,1,0:T(8,128)}, f32[33,64,128]{2,1,0:T(8,128)S(1)}, u32[]{:S(2)}, u32[]{:S(2)}) collective-permute-start(f32[33,64,128]{2,1,0:T(8,128)} %shard_map.46), channel_id=1, source_target_pairs={{0,1},{1,0},{2,3},{3,2},{4,5},{5,4},{6,7},{7,6},{8,9},{9,8},{10,11... | collective-permute-start | bytes 3244040 | tf_op jit(solution)/shard_map/ppermute | solution.py:551
  11.6 7.5 %collective-permute-start.7 = (f32[14,64,128]{2,1,0:T(8,128)S(1)}, f32[14,64,128]{2,1,0:T(8,128)S(1)}, u32[]{:S(2)}, u32[]{:S(2)}) collective-permute-start(f32[14,64,128]{2,1,0:T(8,128)S(1)} %get-tuple-element.65.own), channel_id=1, source_target_pairs={{0,1},{1,0},{2,3},{3,2},{4,5},{5,4},{6,7},{7,6},{8,9},{9,8},{10,11... | collective-permute-start | bytes 1376264 | tf_op jit(solution)/shard_map/ppermute | solution.py:551
  21.2 23.5 %collective-permute-start.8 = (f32[22,64,128]{2,1,0:T(8,128)S(1)}, f32[22,64,128]{2,1,0:T(8,128)S(1)}, u32[]{:S(2)}, u32[]{:S(2)}) collective-permute-start(f32[22,64,128]{2,1,0:T(8,128)S(1)} %shard_map.54), channel_id=1, source_target_pairs={{1,2},{2,1},{3,4},{4,3},{5,6},{6,5},{7,8},{8,7},{9,10},{10,9},{11,... | collective-permute-start | bytes 2162696 | tf_op jit(solution)/shard_map/ppermute | solution.py:557
  22.1 4.5 %collective-permute-start.2 = (f32[14,64,128]{2,1,0:T(8,128)S(1)}, f32[14,64,128]{2,1,0:T(8,128)S(1)}, u32[]{:S(2)}, u32[]{:S(2)}) collective-permute-start(f32[14,64,128]{2,1,0:T(8,128)S(1)} %get-tuple-element.58), channel_id=1, source_target_pairs={{0,1},{1,0},{2,3},{3,2},{4,5},{5,4},{6,7},{7,6},{8,9},{9,8},{10,11... | collective-permute-start | bytes 1376264 | tf_op jit(solution)/shard_map/ppermute | solution.py:551
  25.1 1.4 collective-permute-start.3
  32.3 13.4 %collective-permute-start.4 = (f32[4,64,128]{2,1,0:T(8,128)S(1)}, f32[4,64,128]{2,1,0:T(8,128)S(1)}, u32[]{:S(2)}, u32[]{:S(2)}) collective-permute-start(f32[4,64,128]{2,1,0:T(8,128)S(1)} %get-tuple-element.64.own), channel_id=1, source_target_pairs={{0,1},{1,0},{2,3},{3,2},{4,5},{5,4},{6,7},{7,6},{8,9},{9,8},{10,11... | collective-permute-start | bytes 393224 | tf_op jit(solution)/shard_map/ppermute | solution.py:551
  44.7 9.1 %collective-permute-start.9 = (f32[22,64,128]{2,1,0:T(8,128)S(1)}, f32[22,64,128]{2,1,0:T(8,128)S(1)}, u32[]{:S(2)}, u32[]{:S(2)}) collective-permute-start(f32[22,64,128]{2,1,0:T(8,128)S(1)} %collective-permute-done.8.mine), channel_id=1, source_target_pairs={{0,1},{1,0},{2,3},{3,2},{4,5},{5,4},{6,7},{7,6},{8,9},{9,8},{10,11... | collective-permute-start | bytes 2162696 | tf_op jit(solution)/shard_map/ppermute | solution.py:551
  45.7 0.7 collective-permute-start.5
  46.4 8.5 %collective-permute-start.6 = (f32[8,64,128]{2,1,0:T(8,128)S(1)}, f32[8,64,128]{2,1,0:T(8,128)S(1)}, u32[]{:S(2)}, u32[]{:S(2)}) collective-permute-start(f32[8,64,128]{2,1,0:T(8,128)S(1)} %collective-permute-done.5.mine), channel_id=1, source_target_pairs={{0,1},{1,0},{2,3},{3,2},{4,5},{5,4},{6,7},{7,6},{8,9},{9,8},{10,11... | collective-permute-start | bytes 786440 | tf_op jit(solution)/shard_map/ppermute | solution.py:551
  54.6 22.7 %copy-start.2 = (f32[4,1,28,64,64]{4,3,2,1,0:T(8,128)S(1)}, f32[4,1,28,64,64]{4,3,2,1,0:T(8,128)}, u32[]{:S(2)}) copy-start(f32[4,1,28,64,64]{4,3,2,1,0:T(8,128)} %param.6) | copy-start | bytes 5505028
  56.8 14.5 %collective-permute-start.12 = (f32[2,64,128]{2,1,0:T(8,128)S(1)}, f32[2,64,128]{2,1,0:T(8,128)S(1)}, u32[]{:S(2)}, u32[]{:S(2)}) collective-permute-start(f32[2,64,128]{2,1,0:T(8,128)S(1)} %get-tuple-element.67.own), channel_id=1, source_target_pairs={{0,6},{1,7},{2,0},{3,1},{4,2},{5,3},{6,4},{7,5},{8,14},{9,15},{10,... | collective-permute-start | bytes 196616 | tf_op jit(solution)/shard_map/ppermute | solution.py:575
  65.9 6.0 %collective-permute-start.10 = (f32[2,64,128]{2,1,0:T(8,128)S(1)}, f32[2,64,128]{2,1,0:T(8,128)S(1)}, u32[]{:S(2)}, u32[]{:S(2)}) collective-permute-start(f32[2,64,128]{2,1,0:T(8,128)S(1)} %get-tuple-element.67.own), channel_id=1, source_target_pairs={{0,2},{1,3},{2,4},{3,5},{4,6},{5,7},{6,0},{7,1},{8,10},{9,11},{10,... | collective-permute-start | bytes 196616 | tf_op jit(solution)/shard_map/ppermute | solution.py:575
  65.9 5.4 %collective-permute-start.11 = (f32[1,64,128]{2,1,0:T(8,128)S(1)}, f32[1,64,128]{2,1,0:T(8,128)S(1)}, u32[]{:S(2)}, u32[]{:S(2)}) collective-permute-start(f32[1,64,128]{2,1,0:T(8,128)S(1)} %get-tuple-element.68), channel_id=1, source_target_pairs={{0,4},{1,5},{2,6},{3,7},{4,0},{5,1},{6,2},{7,3},{8,12},{9,13},{10,... | collective-permute-start | bytes 98312 | tf_op jit(solution)/shard_map/ppermute | solution.py:575
  72.0 11.6 %collective-permute-start.15 = (f32[5,64,128]{2,1,0:T(8,128)S(1)}, f32[5,64,128]{2,1,0:T(8,128)S(1)}, u32[]{:S(2)}, u32[]{:S(2)}) collective-permute-start(f32[5,64,128]{2,1,0:T(8,128)S(1)} %get-tuple-element.69.refs_0_), channel_id=1, source_target_pairs={{0,24},{1,25},{2,26},{3,27},{4,28},{5,29},{6,30},{7,31},{8,0},{9,1... | collective-permute-start | bytes 491528 | tf_op jit(solution)/shard_map/ppermute | solution.py:575
  74.3 9.3 %collective-permute-start.13 = (f32[5,64,128]{2,1,0:T(8,128)S(1)}, f32[5,64,128]{2,1,0:T(8,128)S(1)}, u32[]{:S(2)}, u32[]{:S(2)}) collective-permute-start(f32[5,64,128]{2,1,0:T(8,128)S(1)} %get-tuple-element.69.refs_0_), channel_id=1, source_target_pairs={{0,8},{1,9},{2,10},{3,11},{4,12},{5,13},{6,14},{7,15},{8,16},{9,17... | collective-permute-start | bytes 491528 | tf_op jit(solution)/shard_map/ppermute | solution.py:575
  74.3 9.3 %collective-permute-start.14 = (f32[4,64,128]{2,1,0:T(8,128)S(1)}, f32[4,64,128]{2,1,0:T(8,128)S(1)}, u32[]{:S(2)}, u32[]{:S(2)}) collective-permute-start(f32[4,64,128]{2,1,0:T(8,128)S(1)} %get-tuple-element.70), channel_id=1, source_target_pairs={{0,16},{1,17},{2,18},{3,19},{4,20},{5,21},{6,22},{7,23},{8,24},{9,... | collective-permute-start | bytes 393224 | tf_op jit(solution)/shard_map/ppermute | solution.py:575
  91.6 1.8 %collective-permute-start.16 = (f32[11,64,128]{2,1,0:T(8,128)S(1)}, f32[11,64,128]{2,1,0:T(8,128)S(1)}, u32[]{:S(2)}, u32[]{:S(2)}) collective-permute-start(f32[11,64,128]{2,1,0:T(8,128)S(1)} %get-tuple-element.83), channel_id=1, source_target_pairs={{0,1},{1,0},{2,3},{3,2},{4,5},{5,4},{6,7},{7,6},{8,9},{9,8},{10,11... | collective-permute-start | bytes 1081352 | tf_op jit(solution)/shard_map/ppermute | solution.py:551
  91.7 1.7 %collective-permute-start.17 = (f32[11,64,128]{2,1,0:T(8,128)S(1)}, f32[11,64,128]{2,1,0:T(8,128)S(1)}, u32[]{:S(2)}, u32[]{:S(2)}) collective-permute-start(f32[11,64,128]{2,1,0:T(8,128)S(1)} %get-tuple-element.84), channel_id=1, source_target_pairs={{1,2},{2,1},{3,4},{4,3},{5,6},{6,5},{7,8},{8,7},{9,10},{10,9},{11,... | collective-permute-start | bytes 1081352 | tf_op jit(solution)/shard_map/ppermute | solution.py:557
  97.8 8.6 %collective-permute-start.18 = (f32[4,64,128]{2,1,0:T(8,128)S(1)}, f32[4,64,128]{2,1,0:T(8,128)S(1)}, u32[]{:S(2)}, u32[]{:S(2)}) collective-permute-start(f32[4,64,128]{2,1,0:T(8,128)S(1)} %get-tuple-element.86.own), channel_id=1, source_target_pairs={{0,1},{1,0},{2,3},{3,2},{4,5},{5,4},{6,7},{7,6},{8,9},{9,8},{10,11... | collective-permute-start | bytes 393224 | tf_op jit(solution)/shard_map/ppermute | solution.py:551
  106.5 32.9 %copy-start.3 = (s32[1,32]{1,0:T(1,128)S(1)}, s32[1,32]{1,0:T(1,128)}, u32[]{:S(2)}) copy-start(s32[1,32]{1,0:T(1,128)} %refs_0_.1) | copy-start | bytes 388
  106.5 0.7 collective-permute-start.19
  107.2 8.5 %collective-permute-start.20 = (f32[8,64,128]{2,1,0:T(8,128)S(1)}, f32[8,64,128]{2,1,0:T(8,128)S(1)}, u32[]{:S(2)}, u32[]{:S(2)}) collective-permute-start(f32[8,64,128]{2,1,0:T(8,128)S(1)} %collective-permute-done.19.mine), channel_id=1, source_target_pairs={{0,1},{1,0},{2,3},{3,2},{4,5},{5,4},{6,7},{7,6},{8,9},{9,8},{10,11... | collective-permute-start | bytes 786440 | tf_op jit(solution)/shard_map/ppermute | solution.py:551
  117.6 11.3 %collective-permute-start.23 = (f32[2,64,128]{2,1,0:T(8,128)S(1)}, f32[2,64,128]{2,1,0:T(8,128)S(1)}, u32[]{:S(2)}, u32[]{:S(2)}) collective-permute-start(f32[2,64,128]{2,1,0:T(8,128)S(1)} %get-tuple-element.87.own), channel_id=1, source_target_pairs={{0,6},{1,7},{2,0},{3,1},{4,2},{5,3},{6,4},{7,5},{8,14},{9,15},{10,... | collective-permute-start | bytes 196616 | tf_op jit(solution)/shard_map/ppermute | solution.py:575
  123.5 6.0 %collective-permute-start.21 = (f32[2,64,128]{2,1,0:T(8,128)S(1)}, f32[2,64,128]{2,1,0:T(8,128)S(1)}, u32[]{:S(2)}, u32[]{:S(2)}) collective-permute-start(f32[2,64,128]{2,1,0:T(8,128)S(1)} %get-tuple-element.87.own), channel_id=1, source_target_pairs={{0,2},{1,3},{2,4},{3,5},{4,6},{5,7},{6,0},{7,1},{8,10},{9,11},{10,... | collective-permute-start | bytes 196616 | tf_op jit(solution)/shard_map/ppermute | solution.py:575
  123.5 5.4 %collective-permute-start.22 = (f32[1,64,128]{2,1,0:T(8,128)S(1)}, f32[1,64,128]{2,1,0:T(8,128)S(1)}, u32[]{:S(2)}, u32[]{:S(2)}) collective-permute-start(f32[1,64,128]{2,1,0:T(8,128)S(1)} %get-tuple-element.88), channel_id=1, source_target_pairs={{0,4},{1,5},{2,6},{3,7},{4,0},{5,1},{6,2},{7,3},{8,12},{9,13},{10,... | collective-permute-start | bytes 98312 | tf_op jit(solution)/shard_map/ppermute | solution.py:575
  129.5 9.7 %collective-permute-start.26 = (f32[5,64,128]{2,1,0:T(8,128)S(1)}, f32[5,64,128]{2,1,0:T(8,128)S(1)}, u32[]{:S(2)}, u32[]{:S(2)}) collective-permute-start(f32[5,64,128]{2,1,0:T(8,128)S(1)} %get-tuple-element.89.refs_1_), channel_id=1, source_target_pairs={{0,24},{1,25},{2,26},{3,27},{4,28},{5,29},{6,30},{7,31},{8,0},{9,1... | collective-permute-start | bytes 491528 | tf_op jit(solution)/shard_map/ppermute | solution.py:575
  129.8 9.7 %collective-permute-start.24 = (f32[5,64,128]{2,1,0:T(8,128)S(1)}, f32[5,64,128]{2,1,0:T(8,128)S(1)}, u32[]{:S(2)}, u32[]{:S(2)}) collective-permute-start(f32[5,64,128]{2,1,0:T(8,128)S(1)} %get-tuple-element.89.refs_1_), channel_id=1, source_target_pairs={{0,8},{1,9},{2,10},{3,11},{4,12},{5,13},{6,14},{7,15},{8,16},{9,17... | collective-permute-start | bytes 491528 | tf_op jit(solution)/shard_map/ppermute | solution.py:575
  131.6 7.6 %collective-permute-start.25 = (f32[4,64,128]{2,1,0:T(8,128)S(1)}, f32[4,64,128]{2,1,0:T(8,128)S(1)}, u32[]{:S(2)}, u32[]{:S(2)}) collective-permute-start(f32[4,64,128]{2,1,0:T(8,128)S(1)} %get-tuple-element.90), channel_id=1, source_target_pairs={{0,16},{1,17},{2,18},{3,19},{4,20},{5,21},{6,22},{7,23},{8,24},{9,... | collective-permute-start | bytes 393224 | tf_op jit(solution)/shard_map/ppermute | solution.py:575
  147.0 10.3 %collective-permute-start.27 = (f32[8,64,128]{2,1,0:T(8,128)S(1)}, f32[8,64,128]{2,1,0:T(8,128)S(1)}, u32[]{:S(2)}, u32[]{:S(2)}) collective-permute-start(f32[8,64,128]{2,1,0:T(8,128)S(1)} %get-tuple-element.104), channel_id=1, source_target_pairs={{0,32},{32,64},{64,96},{96,0},{1,33},{33,65},{65,97},{97,1},{2,34}... | collective-permute-start | bytes 786440 | tf_op jit(solution)/shard_map/ppermute | solution.py:663
  149.0 13.4 %collective-permute-start.28 = (f32[8,64,128]{2,1,0:T(8,128)S(1)}, f32[8,64,128]{2,1,0:T(8,128)S(1)}, u32[]{:S(2)}, u32[]{:S(2)}) collective-permute-start(f32[8,64,128]{2,1,0:T(8,128)S(1)} %get-tuple-element.105), channel_id=1, source_target_pairs={{0,64},{32,96},{64,0},{96,32},{1,65},{33,97},{65,1},{97,33},{2,66}... | collective-permute-start | bytes 786440 | tf_op jit(solution)/shard_map/ppermute | solution.py:663
  152.6 9.8 %collective-permute-start.29 = (f32[8,64,128]{2,1,0:T(8,128)S(1)}, f32[8,64,128]{2,1,0:T(8,128)S(1)}, u32[]{:S(2)}, u32[]{:S(2)}) collective-permute-start(f32[8,64,128]{2,1,0:T(8,128)S(1)} %get-tuple-element.106), channel_id=1, source_target_pairs={{0,96},{32,0},{64,32},{96,64},{1,97},{33,1},{65,33},{97,65},{2,98}... | collective-permute-start | bytes 786440 | tf_op jit(solution)/shard_map/ppermute | solution.py:663
  (2 other events, 10.8 us)
